TPU v7x, 32 devices: a whole 2x2x4 slice. The times are simulated.
32 devices in a mesh: seq: 4 (over x, core), chan: 8 (over z, y).
Axes of the slice: x: 2, y: 2, z: 4, core: 2. Of those that a mesh axis runs over, the one named last changes fastest.
Arguments:
- d_out: bfloat16 [2048, 8192], P('seq', 'chan'), may hold values from -6 to 6
- w_out: bfloat16 [1024, 8192], P('chan'), may hold values from -0.0625 to 0.0625
- gate: bfloat16 [2048, 1024], P('seq', 'chan'), may hold values from -6 to 6
- inner: bfloat16 [2048, 1024], P('seq', 'chan'), may hold values from -0.125 to 0.125
- filt: bfloat16 [2048, 1024], P('seq', 'chan'), may hold values from -4 to 4
Outputs:
- grad_inner: bfloat16 [2048, 1024], P('seq', 'chan')
- grad_filter: float32 [2048, 1024], P('seq', 'chan')
All inputs are finite; a program needn't handle non-finite values.
Results may differ from a plain program's by a relative error of at most 0.005.
Values may be sent and summed in bfloat16 or wider, within the bound.
No kernel may reach another device: no remote copies, remote signals or barrier semaphores. Data moves between devices by JAX's collectives and lax.ppermute only.
A program may use at most 64 MiB of HBM per device.

v0:
```python
import functools
import math

import jax
import jax.numpy as jnp
import numpy as np
from jax import lax
from jax.experimental import pallas as pl
from jax.experimental.pallas import tpu as pltpu
from jax.sharding import PartitionSpec as P


SUB = 256
LANES = 128
VMEM = pl.BlockSpec(memory_space=pltpu.VMEM)
SMEM = pl.BlockSpec(memory_space=pltpu.SMEM)
F32, BF16 = jnp.float32, jnp.bfloat16
NT = (((1,), (1,)), ((), ()))


def swapped(block, axis, mask):
    size = lax.axis_size(axis)
    return lax.ppermute(block, axis, [(i, i ^ mask) for i in range(size)])


def dft_parts():
    freq = np.arange(SUB)[:, None]
    place = np.arange(SUB)[None, :]
    angle = (((2 * freq + 1) * place) % (4 * SUB)).astype(np.float64) * (math.pi / (2 * SUB))
    matrix = np.concatenate([np.cos(angle), -np.sin(angle)], axis=0).astype(np.float32)
    upper = matrix.astype(jnp.bfloat16)
    lower = (matrix - upper.astype(np.float32)).astype(jnp.bfloat16)
    return np.concatenate([upper, lower], axis=0), np.concatenate([upper.T, lower.T], axis=0)


def dot(a, b):
    return jnp.dot(a, b, preferred_element_type=F32)


def dot_parts(parts_ref, b):
    both = dot(parts_ref[...], b)
    half = both.shape[0] // 2
    return both[:half] + both[half:]


def prepare_kernel(widths, start_ref, w_ref, *refs):
    outs, sems = refs[:-1], refs[-1]
    copies = [
        pltpu.make_async_copy(
            w_ref.at[:, pl.ds(pl.multiple_of(start_ref[i], LANES), width)], outs[i], sems.at[i]
        )
        for i, width in enumerate(widths)
    ]
    for copy in copies:
        copy.start()
    for copy in copies:
        copy.wait()


def prepare(w_out, starts, widths):
    rows = w_out.shape[0]
    return pl.pallas_call(
        functools.partial(prepare_kernel, widths),
        out_shape=[jax.ShapeDtypeStruct((rows, width), w_out.dtype) for width in widths],
        in_specs=[SMEM, pl.BlockSpec(memory_space=pltpu.HBM)],
        out_specs=[VMEM] * len(widths),
        scratch_shapes=[pltpu.SemaphoreType.DMA((len(widths),))],
        compiler_params=pltpu.CompilerParams(vmem_limit_bytes=GRANT[0] << 20),
        cost_estimate=pl.CostEstimate(flops=0, bytes_accessed=4 << 20, transcendentals=0),
    )(jnp.stack(starts).astype(jnp.int32), w_out)


PIECES = 4


def hold_kernel(source_ref, out_ref, sems):
    rows = source_ref.shape[0] // PIECES
    copies = [
        pltpu.make_async_copy(source_ref.at[pl.ds(i * rows, rows)], out_ref.at[pl.ds(i * rows, rows)], sems.at[i])
        for i in range(PIECES)
    ]
    for copy in copies:
        copy.start()
    for copy in copies:
        copy.wait()


def hold(block):
    return pl.pallas_call(
        hold_kernel,
        out_shape=jax.ShapeDtypeStruct(block.shape, block.dtype),
        in_specs=[pl.BlockSpec(memory_space=pltpu.HBM)],
        out_specs=VMEM,
        scratch_shapes=[pltpu.SemaphoreType.DMA((PIECES,))],
        compiler_params=pltpu.CompilerParams(vmem_limit_bytes=GRANT[1] << 20),
        cost_estimate=pl.CostEstimate(flops=0, bytes_accessed=2 << 20, transcendentals=0),
    )(block)


def product_kernel(sizes, place_ref, d_ref, *refs):
    parts, outs = refs[: len(sizes)], refs[len(sizes) :]
    count = outs[0].shape[0]
    channels = outs[0].shape[-1]
    for i in range(0, count, 2):
        total = None
        for n, (part, (index, first, masks)) in enumerate(zip(parts, sizes)):
            if not first <= i < first + masks:
                continue
            width = part.shape[-1]
            start = pl.multiple_of(place_ref[n], width)
            w = jnp.concatenate([part[(*index, i - first)], part[(*index, i + 1 - first)]], axis=0)
            term = lax.dot_general(d_ref[:, pl.ds(start, width)], w, NT, preferred_element_type=F32)
            total = term if total is None else total + term
        for which in range(2):
            rows = slice(which * SUB, (which + 1) * SUB)
            outs[which][i] = total[rows, :channels].astype(outs[which].dtype)
            outs[which][i + 1] = total[rows, channels:].astype(outs[which].dtype)


def product(d_out, parts, out_type):
    count = max(first + block.shape[-3] for block, _, first, _ in parts)
    channels = parts[0][0].shape[-2]
    sizes = [(index, first, block.shape[-3]) for block, index, first, _ in parts]
    places = jnp.stack([start for _, _, _, start in parts]).astype(jnp.int32)
    return pl.pallas_call(
        functools.partial(product_kernel, sizes),
        out_shape=(jax.ShapeDtypeStruct((count, SUB, channels), out_type),) * 2,
        in_specs=[SMEM] + [VMEM] * (1 + len(parts)),
        out_specs=(VMEM, VMEM),
        compiler_params=pltpu.CompilerParams(vmem_limit_bytes=8 << 20),
        cost_estimate=pl.CostEstimate(
            flops=4 * count * SUB * channels * d_out.shape[1], bytes_accessed=4 << 20, transcendentals=0
        ),
    )(places, d_out, *[block for block, _, _, _ in parts])


def lag_kernel(n, seq_ref, dft_ref, *refs):
    blocks, out_ref, spec = refs[:n], refs[n], refs[n + 1]
    me = seq_ref[0]
    spec[0] = jnp.zeros_like(spec[0])
    out_ref[0] = jnp.zeros_like(out_ref[0])
    for offset in range(n):
        place = (me ^ offset) * 2 + 1
        for sub in range(2):
            rows = pl.ds(sub * SUB, SUB)
            data = jnp.concatenate([blocks[offset][0, rows, :], blocks[offset][1, rows, :]], axis=1)
            both = dot_parts(dft_ref, data)
            channels = data.shape[1] // 2
            spec[place + sub, 0] = both[:, :channels] * (1.0 / SUB)
            spec[place + sub, 1] = both[:, channels:] * (1.0 / SUB)
    channels = spec.shape[-1]
    sign = (1 - 2 * (lax.broadcasted_iota(jnp.int32, (SUB, channels), 0) % 2)).astype(F32)

    @pl.loop(0, 2 * n)
    def _(lag):
        for which in range(2):
            out_ref[lag + 1, which, :SUB] = spec[lag + 1, which, :SUB] - sign * spec[lag, which, SUB:]
            out_ref[lag + 1, which, SUB:] = spec[lag + 1, which, SUB:] + sign * spec[lag, which, :SUB]


def lag_spectra(seq_id, dft, blocks):
    n = len(blocks)
    channels = blocks[0].shape[-1]
    return pl.pallas_call(
        functools.partial(lag_kernel, n),
        out_shape=jax.ShapeDtypeStruct((2 * n + 1, 2, 2 * SUB, channels), F32),
        in_specs=[SMEM] + [VMEM] * (1 + n),
        out_specs=VMEM,
        scratch_shapes=[pltpu.VMEM((2 * n + 1, 2, 2 * SUB, channels), F32)],
        compiler_params=pltpu.CompilerParams(vmem_limit_bytes=(4 + 3 * n) << 20),
        cost_estimate=pl.CostEstimate(
            flops=16 * n * SUB * SUB * channels * 2, bytes_accessed=6 << 20, transcendentals=0
        ),
    )(seq_id, dft, *blocks)


CHUNK = 32
GRANT = (51, 52)


def add_kernel(offsets, which, first, last, seq_ref, dft_ref, lag_ref, *refs):
    blocks, refs = refs[: len(offsets)], list(refs[len(offsets) :])
    before = None if first else refs.pop(0)
    if last:
        back_ref, inner_ref, filter_ref, spec, total = refs
    else:
        total, spec = refs
    me = seq_ref[0]
    channels = spec.shape[-1]
    for pair in range(0, len(offsets), 2):
        used = offsets[pair : pair + 2]
        data = jnp.concatenate([blocks[pair + i][...] for i in range(len(used))], axis=1)
        both = dot_parts(dft_ref, data)
        for i in range(len(used)):
            spec[pair + i] = both[:, i * channels : (i + 1) * channels]

    for chunk in range(SUB // CHUNK):
        real, imag = pl.ds(chunk * CHUNK, CHUNK), pl.ds(SUB + chunk * CHUNK, CHUNK)
        sums = []
        for i in range(4):
            columns = slice(i * channels, (i + 1) * channels)
            zero = jnp.zeros((CHUNK, channels), F32)
            sums.append((zero, zero) if first else (before[real, columns], before[imag, columns]))
        for place, offset in enumerate(offsets):
            step = (me ^ offset) - me
            g_real, g_imag = spec[place, real, :], spec[place, imag, :]
            for i in range(4):
                array, sub = i // 2, i % 2
                lag = jnp.maximum(step * 2 + which - sub + 1, 0)
                k_real, k_imag = lag_ref[lag, array, real, :], lag_ref[lag, array, imag, :]
                s_real, s_imag = sums[i]
                s_real = s_real + g_real * k_real + g_imag * k_imag
                s_imag = s_imag + g_imag * k_real - g_real * k_imag
                sums[i] = (s_real, s_imag)
        for i in range(4):
            total[real, i * channels : (i + 1) * channels] = sums[i][0]
            total[imag, i * channels : (i + 1) * channels] = sums[i][1]
    if not last:
        return
    for array in range(2):
        whole = total[:, 2 * array * channels : 2 * (array + 1) * channels]
        high = whole.astype(BF16)
        low = (whole - high.astype(F32)).astype(BF16)
        values = dot_parts(back_ref, high) + dot(back_ref[:SUB, :], low)
        out_ref = (inner_ref, filter_ref)[array]
        out_ref[:SUB, :] = values[:, :channels].astype(out_ref.dtype)
        out_ref[SUB:, :] = values[:, channels:].astype(out_ref.dtype)


def add_blocks(n, seq_id, dft, lags, blocks, which, before=None, back=None):
    offsets = sorted(blocks)
    blocks = [blocks[offset] for offset in offsets]
    channels = blocks[0].shape[-1]
    first, last = before is None, back is not None
    whole = jax.ShapeDtypeStruct((2 * SUB, 4 * channels), F32)
    out_shape = whole
    scratch = [pltpu.VMEM((len(blocks), 2 * SUB, channels), F32)]
    if last:
        out_shape = (
            jax.ShapeDtypeStruct((2 * SUB, channels), BF16),
            jax.ShapeDtypeStruct((2 * SUB, channels), F32),
        )
        scratch.append(pltpu.VMEM(whole.shape, F32))
    args = (seq_id, dft, lags, *blocks) + (() if first else (before,)) + ((back,) if last else ())
    return pl.pallas_call(
        functools.partial(add_kernel, offsets, which, first, last),
        out_shape=out_shape,
        in_specs=[SMEM] + [VMEM] * (len(args) - 1),
        out_specs=(VMEM, VMEM) if last else VMEM,
        scratch_shapes=scratch,
        compiler_params=pltpu.CompilerParams(vmem_limit_bytes=(6 + 2 * n) << 20),
        cost_estimate=pl.CostEstimate(
            flops=8 * len(blocks) * SUB * SUB * channels * 2, bytes_accessed=4 << 20, transcendentals=0
        ),
    )(*args)


def spread_offsets(size):
    held, moves, mask = [0], [], size // 2
    while mask:
        new = [(offset | mask, offset, mask) for offset in held]
        moves += new
        held += [offset for offset, _, _ in new]
        mask //= 2
    return moves


def spread_blocks(block, axis):
    size = lax.axis_size(axis)
    held = {0: block}
    for offset, source, mask in spread_offsets(size):
        held[offset] = swapped(held[source], axis, mask)
    return held


def masks_of(chan_n):
    odd = [m for m in reversed(range(chan_n)) if m % 2]
    return odd, [m - 1 for m in odd]


def far_count(chan_n, features):
    return chan_n // 4 if features % (4 * LANES) == 0 else 0


def body(d_out, w_out, gate, inner, filt):
    chan_n = lax.axis_size("chan")
    seq, chan = lax.axis_index("seq"), lax.axis_index("chan")
    core, side = seq % 2, seq // 2 % 2
    seq_id = seq.astype(jnp.int32)[None]
    features = d_out.shape[1]
    half, quarter = features // 2, features // 4
    odd, even = masks_of(chan_n)
    groups = chan_n // 2
    far = far_count(chan_n, features)

    def place(mask, split):
        return (chan ^ mask) * features + core * half + (side * quarter if split else 0)

    splits = [i < far for i in range(groups)]
    starts = [place(mask, split) for mask, split in zip(odd + even, splits + [False] * groups)]
    starts.append(chan * features + (1 - core) * half)
    blocks = list(prepare(w_out, starts, [quarter if split else half for split in splits] + [half] * (groups + 1)))
    d_out = hold(d_out)
    for i, mask in enumerate(odd + even[:-1]):
        blocks[i] = swapped(blocks[i], "chan", mask)
    odd_parts, even_parts = [], []
    if far:
        own = jnp.stack(blocks[:far])
        own = jnp.stack([own, swapped(own, "seq", 2)])
        twin = swapped(own, "seq", 1)
        for other_core, block in enumerate((own, twin)):
            for other_side in range(2):
                start = (core ^ other_core) * half + (side ^ other_side) * quarter
                odd_parts.append((block, (other_side,), 0, start))
    near = jnp.stack(blocks[far:groups])
    twin = swapped(near, "seq", 1)
    odd_parts += [(near, (), far, core * half), (twin, (), far, (1 - core) * half)]
    lag_pair = jnp.stack([filt, inner])
    lag_blocks = [block for _, block in sorted(spread_blocks(lag_pair, "seq").items())]
    dft, back = dft_parts()

    p_odd = product(d_out, odd_parts, BF16)
    *later, _ = lax.optimization_barrier((*blocks[groups : 2 * groups - 1], p_odd[0]))
    near = jnp.stack(later)
    twin = swapped(near, "seq", 1)
    even_parts = [
        (jnp.concatenate([near, blocks[-2][None]]), (), 0, core * half),
        (jnp.concatenate([twin, blocks[-1][None]]), (), 0, (1 - core) * half),
    ]
    from_pair = [swapped(p_odd[which], "chan", 1) for which in range(2)]
    lags = lag_spectra(seq_id, dft, lag_blocks)
    p_even = product(d_out, even_parts, F32)
    sums, sent = [], []
    for which in range(2):
        sums.append([p_even[which][i] + from_pair[which][i].astype(F32) for i in range(groups)])
        sent.append([block.astype(BF16) for block in sums[which][:-1]])
    parts = [[swapped(block, "chan", mask) for block, mask in zip(sent[which], even)] for which in range(2)]
    tied = lax.optimization_barrier((*parts[0], *sent[1]))
    parts[0] = list(tied[: groups - 1])
    grad_blocks = []
    for which in range(2):
        grad_gated = sums[which][-1]
        for part in parts[which]:
            grad_gated = grad_gated + part.astype(F32)
        gate_part = gate[which * SUB : (which + 1) * SUB].astype(F32)
        grad_conv = (gate_part * grad_gated).astype(BF16)
        gate, grad_conv = lax.optimization_barrier((gate, grad_conv))
        grad_blocks.append(spread_blocks(grad_conv, "seq"))
    seq_n = lax.axis_size("seq")
    groups_of = stages(seq_n)
    total = None
    for i, (which, offsets) in enumerate(groups_of):
        last = i == len(groups_of) - 1
        chosen = {offset: grad_blocks[which][offset] for offset in offsets}
        total = add_blocks(seq_n, seq_id, dft, lags, chosen, which, total, back if last else None)
    return tuple(total)


def stages(seq_n):
    near = [0, 1] if seq_n > 1 else [0]
    rest = [offset for offset in range(seq_n) if offset not in near]
    return [(0, list(range(seq_n))), (1, near)] + ([(1, rest)] if rest else [])


def solution(mesh):
    placed = (
        P("seq", "chan"),
        P("chan", None),
        P("seq", "chan"),
        P("seq", "chan"),
        P("seq", "chan"),
    )

    return jax.shard_map(
        body,
        mesh=mesh,
        in_specs=placed,
        out_specs=(P("seq", "chan"), P("seq", "chan")),
        check_vma=False,
    )
```

profile of v0, /device:TPU:0, one launch (start us, length us, event | category | flops | bytes accessed | tf_op | source)
XLA Modules:
  0.0 76.4 jit_solution(12573850502359886670)
XLA Ops:
  0.8 1.9 %shard_map.88 = (bf16[128,256]{1,0:T(8,128)(2,1)S(1)}, bf16[128,256]{1,0:T(8,128)(2,1)S(1)}, bf16[128,512]{1,0:T(8,128)(2,1)S(1)}, bf16[128,512]{1,0:T(8,128)(2,...) custom-call(s32[9]{0:T(128)S(1)} %stack.119.start_ref, ...), custom_call_target="tpu_custom_call" | custom-call | bytes 4194304 | tf_op jit(solution)/shard_map/pallas_call | solution.py:62
  2.7 6.1 %collective-permute-start.6 = (bf16[128,256]{1,0:T(8,128)(2,1)S(1)}, bf16[128,256]{1,0:T(8,128)(2,1)S(1)}, u32[]{:S(2)}, u32[]{:S(2)}) collective-permute-start(bf16[128,256]{1,0:T(8,128)(2,1)S(1)} %get-tuple-element.27), channel_id=1, source_target_pairs={{0,7},{1,6},{2,5},{3,4},{4,3},{5,2},{6,1},{7,0},{8,15},{9,14},{10,... | collective-permute-start | bytes 196616 | tf_op jit(solution)/shard_map/ppermute | solution.py:23
  8.8 1.7 %collective-permute-start.10 = (bf16[128,512]{1,0:T(8,128)(2,1)S(1)}, bf16[128,512]{1,0:T(8,128)(2,1)S(1)}, u32[]{:S(2)}, u32[]{:S(2)}) collective-permute-start(bf16[128,512]{1,0:T(8,128)(2,1)S(1)} %get-tuple-element.29), channel_id=1, source_target_pairs={{0,3},{1,2},{2,1},{3,0},{4,7},{5,6},{6,5},{7,4},{8,11},{9,10},{10,... | collective-permute-start | bytes 393224 | tf_op jit(solution)/shard_map/ppermute | solution.py:23
  11.3 3.7 %collective-permute-done.7 = bf16[128,256]{1,0:T(8,128)(2,1)S(1)} collective-permute-done((bf16[128,256]{1,0:T(8,128)(2,1)S(1)}, bf16[128,256]{1,0:T(8,128)(2,1)S(1)}, u32[]{:S(2)}, u32[]{:S(2)}) %collective-permute-start.7) | collective-permute-done | bytes 65568 | tf_op jit(solution)/shard_map/ppermute | solution.py:23
  15.1 1.6 %collective-permute-start.8 = (bf16[2,128,256]{2,1,0:T(8,128)(2,1)S(1)}, bf16[2,128,256]{2,1,0:T(8,128)(2,1)S(1)}, u32[]{:S(2)}, u32[]{:S(2)}) collective-permute-start(bf16[2,128,256]{2,1,0:T(8,128)(2,1)S(1)} %get-tuple-element.53), channel_id=1, source_target_pairs={{0,16},{8,24},{16,0},{24,8},{1,17},{9,25},{17,1},{25,9},{2,18},{10... | collective-permute-start | bytes 393224 | tf_op jit(solution)/shard_map/ppermute | solution.py:23
  16.6 2.3 %collective-permute-done.11 = bf16[128,512]{1,0:T(8,128)(2,1)S(1)} collective-permute-done((bf16[128,512]{1,0:T(8,128)(2,1)S(1)}, bf16[128,512]{1,0:T(8,128)(2,1)S(1)}, u32[]{:S(2)}, u32[]{:S(2)}) %collective-permute-start.11) | collective-permute-done | bytes 131104 | tf_op jit(solution)/shard_map/ppermute | solution.py:23
  19.0 1.1 %collective-permute-done.8 = bf16[2,128,256]{2,1,0:T(8,128)(2,1)S(1)} collective-permute-done((bf16[2,128,256]{2,1,0:T(8,128)(2,1)S(1)}, bf16[2,128,256]{2,1,0:T(8,128)(2,1)S(1)}, u32[]{:S(2)}, u32[]{:S(2)}) %collective-permute-start.8) | collective-permute-done | bytes 131104 | tf_op jit(solution)/shard_map/ppermute | solution.py:23
  20.2 2.7 %collective-permute-start.3 = (bf16[128,512]{1,0:T(8,128)(2,1)S(1)}, bf16[128,512]{1,0:T(8,128)(2,1)S(1)}, u32[]{:S(2)}, u32[]{:S(2)}) collective-permute-start(bf16[128,512]{1,0:T(8,128)(2,1)S(1)} %get-tuple-element.24), channel_id=1, source_target_pairs={{0,6},{1,7},{2,4},{3,5},{4,2},{5,3},{6,0},{7,1},{8,14},{9,15},{10,... | collective-permute-start | bytes 393224 | tf_op jit(solution)/shard_map/ppermute | solution.py:23
  22.9 1.8 %collective-permute-start.5 = (bf16[128,512]{1,0:T(8,128)(2,1)S(1)}, bf16[128,512]{1,0:T(8,128)(2,1)S(1)}, u32[]{:S(2)}, u32[]{:S(2)}) collective-permute-start(bf16[128,512]{1,0:T(8,128)(2,1)S(1)} %get-tuple-element.26), channel_id=1, source_target_pairs={{0,2},{1,3},{2,0},{3,1},{4,6},{5,7},{6,4},{7,5},{8,10},{9,11},{10,... | collective-permute-start | bytes 393224 | tf_op jit(solution)/shard_map/ppermute | solution.py:23
  24.7 1.2 %shard_map.87.d_ref = bf16[512,1024]{1,0:T(8,128)(2,1)S(1)} custom-call(bf16[512,1024]{1,0:T(8,128)(2,1)} %source_ref.1), custom_call_target="tpu_custom_call" | custom-call | bytes 2097152 | tf_op jit(solution)/shard_map/pallas_call | solution.py:89
  26.0 1.3 %shard_map.89 = (bf16[4,256,128]{2,1,0:T(8,128)(2,1)S(1)}, bf16[4,256,128]{2,1,0:T(8,128)(2,1)S(1)}) custom-call(s32[6]{0:T(128)S(1)} %stack.124.place_ref, bf16[512,1024]{1,0:T(8,128)(2,1)S(1)} %shard_map.87.d_ref, bf16[2,2,128,256]{3,2,1,0:T(8,128)(2,1)S(1)} %pad_maximum_fusion.4.refs_0_.refs_1_, ...), custom_call_target="tpu_custom_call" | custom-call | flops 536870912 | bytes 4194304 | tf_op jit(solution)/shard_map/pallas_call | solution.py:125
  27.3 1.3 %collective-permute-done.3 = bf16[128,512]{1,0:T(8,128)(2,1)S(1)} collective-permute-done((bf16[128,512]{1,0:T(8,128)(2,1)S(1)}, bf16[128,512]{1,0:T(8,128)(2,1)S(1)}, u32[]{:S(2)}, u32[]{:S(2)}) %collective-permute-start.3) | collective-permute-done | bytes 131104 | tf_op jit(solution)/shard_map/ppermute | solution.py:23
  28.6 5.8 %collective-permute-done.4 = bf16[128,512]{1,0:T(8,128)(2,1)S(1)} collective-permute-done((bf16[128,512]{1,0:T(8,128)(2,1)S(1)}, bf16[128,512]{1,0:T(8,128)(2,1)S(1)}, u32[]{:S(2)}, u32[]{:S(2)}) %collective-permute-start.4) | collective-permute-done | bytes 131104 | tf_op jit(solution)/shard_map/ppermute | solution.py:23
  34.6 1.6 %collective-permute-start.1 = (bf16[2,512,128]{2,1,0:T(8,128)(2,1)S(1)}, bf16[2,512,128]{2,1,0:T(8,128)(2,1)S(1)}, u32[]{:S(2)}, u32[]{:S(2)}) collective-permute-start(bf16[2,512,128]{2,1,0:T(8,128)(2,1)S(1)} %pad_maximum_fusion.3.refs_0_), channel_id=1, source_target_pairs={{0,16},{8,24},{16,0},{24,8},{1,17},{9,25},{17,1},{25,9},{2,18},{10... | collective-permute-start | bytes 786440 | tf_op jit(solution)/shard_map/ppermute | solution.py:23
  36.4 6.9 %collective-permute-done.1.refs_2_ = bf16[2,512,128]{2,1,0:T(8,128)(2,1)S(1)} collective-permute-done((bf16[2,512,128]{2,1,0:T(8,128)(2,1)S(1)}, bf16[2,512,128]{2,1,0:T(8,128)(2,1)S(1)}, u32[]{:S(2)}, u32[]{:S(2)}) %collective-permute-start.1) | collective-permute-done | bytes 262176 | tf_op jit(solution)/shard_map/ppermute | solution.py:23
  43.4 1.6 %collective-permute-start.14 = (bf16[4,256,128]{2,1,0:T(8,128)(2,1)S(1)}, bf16[4,256,128]{2,1,0:T(8,128)(2,1)S(1)}, u32[]{:S(2)}, u32[]{:S(2)}) collective-permute-start(bf16[4,256,128]{2,1,0:T(8,128)(2,1)S(1)} %get-tuple-element.31), channel_id=1, source_target_pairs={{0,1},{1,0},{2,3},{3,2},{4,5},{5,4},{6,7},{7,6},{8,9},{9,8},{10,11... | collective-permute-start | bytes 786440 | tf_op jit(solution)/shard_map/ppermute | solution.py:23
  45.5 1.3 %shard_map.90 = (f32[4,256,128]{2,1,0:T(8,128)S(1)}, f32[4,256,128]{2,1,0:T(8,128)S(1)}) custom-call(s32[2]{0:T(128)S(1)} %pad_add_fusion.place_ref, bf16[512,1024]{1,0:T(8,128)(2,1)S(1)} %shard_map.87.d_ref, bf16[4,128,512]{2,1,0:T(8,128)(2,1)S(1)} %pad_maximum_fusion.refs_0_, bf16[4,128,512]{2,1,0:T(8,128)(2,1)S(1)} %pad_maximum_fusion.1.refs_1_), custom_call_target="tpu_custom_call" | custom-call | flops 536870912 | bytes 4194304 | tf_op jit(solution)/shard_map/pallas_call | solution.py:125
  46.8 5.7 %collective-permute-done.14 = bf16[4,256,128]{2,1,0:T(8,128)(2,1)S(1)} collective-permute-done((bf16[4,256,128]{2,1,0:T(8,128)(2,1)S(1)}, bf16[4,256,128]{2,1,0:T(8,128)(2,1)S(1)}, u32[]{:S(2)}, u32[]{:S(2)}) %collective-permute-start.14) | collective-permute-done | bytes 262176 | tf_op jit(solution)/shard_map/ppermute | solution.py:23
  52.6 2.7 %collective-permute-start.15 = (bf16[256,128]{1,0:T(8,128)(2,1)S(1)}, bf16[256,128]{1,0:T(8,128)(2,1)S(1)}, u32[]{:S(2)}, u32[]{:S(2)}) collective-permute-start(bf16[256,128]{1,0:T(8,128)(2,1)S(1)} %get-tuple-element.51), channel_id=1, source_target_pairs={{0,6},{1,7},{2,4},{3,5},{4,2},{5,3},{6,0},{7,1},{8,14},{9,15},{10,... | collective-permute-start | bytes 196616 | tf_op jit(solution)/shard_map/ppermute | solution.py:23
  55.3 2.4 %collective-permute-done.18 = bf16[4,256,128]{2,1,0:T(8,128)(2,1)S(1)} collective-permute-done((bf16[4,256,128]{2,1,0:T(8,128)(2,1)S(1)}, bf16[4,256,128]{2,1,0:T(8,128)(2,1)S(1)}, u32[]{:S(2)}, u32[]{:S(2)}) %collective-permute-start.18) | collective-permute-done | bytes 262176 | tf_op jit(solution)/shard_map/ppermute | solution.py:23
  57.8 1.0 %collective-permute-done.15 = bf16[256,128]{1,0:T(8,128)(2,1)S(1)} collective-permute-done((bf16[256,128]{1,0:T(8,128)(2,1)S(1)}, bf16[256,128]{1,0:T(8,128)(2,1)S(1)}, u32[]{:S(2)}, u32[]{:S(2)}) %collective-permute-start.15) | collective-permute-done | bytes 65568 | tf_op jit(solution)/shard_map/ppermute | solution.py:23
  58.7 2.6 %collective-permute-start.19 = (bf16[256,128]{1,0:T(8,128)(2,1)S(1)}, bf16[256,128]{1,0:T(8,128)(2,1)S(1)}, u32[]{:S(2)}, u32[]{:S(2)}) collective-permute-start(bf16[256,128]{1,0:T(8,128)(2,1)S(1)} %get-tuple-element.48), channel_id=1, source_target_pairs={{0,6},{1,7},{2,4},{3,5},{4,2},{5,3},{6,0},{7,1},{8,14},{9,15},{10,... | collective-permute-start | bytes 196616 | tf_op jit(solution)/shard_map/ppermute | solution.py:23
  61.4 0.7 collective-permute-done.17
  62.1 1.6 %collective-permute-start.21 = (bf16[256,128]{1,0:T(8,128)(2,1)S(1)}, bf16[256,128]{1,0:T(8,128)(2,1)S(1)}, u32[]{:S(2)}, u32[]{:S(2)}) collective-permute-start(bf16[256,128]{1,0:T(8,128)(2,1)S(1)} %get-tuple-element.46), channel_id=1, source_target_pairs={{0,2},{1,3},{2,0},{3,1},{4,6},{5,7},{6,4},{7,5},{8,10},{9,11},{10,... | collective-permute-start | bytes 196616 | tf_op jit(solution)/shard_map/ppermute | solution.py:23
  63.8 1.6 %collective-permute-done.19 = bf16[256,128]{1,0:T(8,128)(2,1)S(1)} collective-permute-done((bf16[256,128]{1,0:T(8,128)(2,1)S(1)}, bf16[256,128]{1,0:T(8,128)(2,1)S(1)}, u32[]{:S(2)}, u32[]{:S(2)}) %collective-permute-start.19) | collective-permute-done | bytes 65568 | tf_op jit(solution)/shard_map/ppermute | solution.py:23
  65.4 1.5 %collective-permute-start.26 = (bf16[256,128]{1,0:T(8,128)(2,1)S(1)}, bf16[256,128]{1,0:T(8,128)(2,1)S(1)}, u32[]{:S(2)}, u32[]{:S(2)}) collective-permute-start(bf16[256,128]{1,0:T(8,128)(2,1)S(1)} %fusion.7.refs_0_), channel_id=1, source_target_pairs={{0,16},{8,24},{16,0},{24,8},{1,17},{9,25},{17,1},{25,9},{2,18},{10... | collective-permute-start | bytes 196616 | tf_op jit(solution)/shard_map/ppermute | solution.py:23
  67.9 1.5 %collective-permute-start.22 = (bf16[256,128]{1,0:T(8,128)(2,1)S(1)}, bf16[256,128]{1,0:T(8,128)(2,1)S(1)}, u32[]{:S(2)}, u32[]{:S(2)}) collective-permute-start(bf16[256,128]{1,0:T(8,128)(2,1)S(1)} %fusion.3.refs_0_), channel_id=1, source_target_pairs={{0,16},{8,24},{16,0},{24,8},{1,17},{9,25},{17,1},{25,9},{2,18},{10... | collective-permute-start | bytes 196616 | tf_op jit(solution)/shard_map/ppermute | solution.py:23
  69.7 1.7 %shard_map.86.lag_ref = f32[9,2,512,128]{3,2,1,0:T(8,128)S(1)} custom-call(s32[1]{0:T(128)} %bitcast.seq_ref, bf16[1024,256]{1,0:T(8,128)(2,1)S(1)} %copy-done, bf16[2,512,128]{2,1,0:T(8,128)(2,1)S(1)} %pad_maximum_fusion.3.refs_0_, bf16[2,512,128]{2,1,0:T(8,128)(2,1)S(1)} %collective-permute-done.refs_1_, ...), custom_call_target="tpu_custom_call" | custom-call | flops 1073741824 | bytes 6291456 | tf_op jit(solution)/shard_map/pallas_call | solution.py:164
  71.4 0.8 %collective-permute-done.22.refs_0_ = bf16[256,128]{1,0:T(8,128)(2,1)S(1)} collective-permute-done((bf16[256,128]{1,0:T(8,128)(2,1)S(1)}, bf16[256,128]{1,0:T(8,128)(2,1)S(1)}, u32[]{:S(2)}, u32[]{:S(2)}) %collective-permute-start.22) | collective-permute-done | bytes 65568 | tf_op jit(solution)/shard_map/ppermute | solution.py:23
  72.2 1.3 %shard_map.91.refs_2_ = f32[512,512]{1,0:T(8,128)S(1)} custom-call(s32[1]{0:T(128)} %bitcast.seq_ref, bf16[1024,256]{1,0:T(8,128)(2,1)S(1)} %copy-done, f32[9,2,512,128]{3,2,1,0:T(8,128)S(1)} %shard_map.86.lag_ref, bf16[256,128]{1,0:T(8,128)(2,1)S(1)} %fusion.7.refs_0_, bf16[256,128]{1,0:T(8,128)(2,1)S(1)} %collective-permute-done.25.refs_1_, ...), custom_call_target="tpu_custom_call" | custom-call | flops 536870912 | bytes 4194304 | tf_op jit(solution)/shard_map/pallas_call | solution.py:245
  73.5 0.7 shard_map.92.refs_2_
  74.6 1.8 %shard_map.93 = (bf16[512,128]{1,0:T(8,128)(2,1)}, f32[512,128]{1,0:T(8,128)}) custom-call(s32[1]{0:T(128)} %bitcast.seq_ref, bf16[1024,256]{1,0:T(8,128)(2,1)S(1)} %copy-done, f32[9,2,512,128]{3,2,1,0:T(8,128)S(1)} %shard_map.86.lag_ref, bf16[256,128]{1,0:T(8,128)(2,1)S(1)} %collective-permute-done.22.refs_0_, ...), custom_call_target="tpu_custom_call" | custom-call | flops 268435456 | bytes 4194304 | tf_op jit(solution)/shard_map/pallas_call | solution.py:245
  (56 shorter events, 4.0 us)
Async XLA Ops:
  0.6 33.9 %copy-start.3 = (bf16[512,128]{1,0:T(8,128)(2,1)S(1)}, bf16[512,128]{1,0:T(8,128)(2,1)}, u32[]{:S(2)}) copy-start(bf16[512,128]{1,0:T(8,128)(2,1)} %param.11) | copy-start | bytes 393220
  0.6 33.9 %copy-start.2 = (bf16[512,128]{1,0:T(8,128)(2,1)S(1)}, bf16[512,128]{1,0:T(8,128)(2,1)}, u32[]{:S(2)}) copy-start(bf16[512,128]{1,0:T(8,128)(2,1)} %param.10) | copy-start | bytes 393220
  2.7 8.6 %collective-permute-start.6 = (bf16[128,256]{1,0:T(8,128)(2,1)S(1)}, bf16[128,256]{1,0:T(8,128)(2,1)S(1)}, u32[]{:S(2)}, u32[]{:S(2)}) collective-permute-start(bf16[128,256]{1,0:T(8,128)(2,1)S(1)} %get-tuple-element.27), channel_id=1, source_target_pairs={{0,7},{1,6},{2,5},{3,4},{4,3},{5,2},{6,1},{7,0},{8,15},{9,14},{10,... | collective-permute-start | bytes 196616 | tf_op jit(solution)/shard_map/ppermute | solution.py:23
  8.8 6.2 %collective-permute-start.7 = (bf16[128,256]{1,0:T(8,128)(2,1)S(1)}, bf16[128,256]{1,0:T(8,128)(2,1)S(1)}, u32[]{:S(2)}, u32[]{:S(2)}) collective-permute-start(bf16[128,256]{1,0:T(8,128)(2,1)S(1)} %get-tuple-element.28), channel_id=1, source_target_pairs={{0,5},{1,4},{2,7},{3,6},{4,1},{5,0},{6,3},{7,2},{8,13},{9,12},{10,... | collective-permute-start | bytes 196616 | tf_op jit(solution)/shard_map/ppermute | solution.py:23
  8.8 7.8 %collective-permute-start.10 = (bf16[128,512]{1,0:T(8,128)(2,1)S(1)}, bf16[128,512]{1,0:T(8,128)(2,1)S(1)}, u32[]{:S(2)}, u32[]{:S(2)}) collective-permute-start(bf16[128,512]{1,0:T(8,128)(2,1)S(1)} %get-tuple-element.29), channel_id=1, source_target_pairs={{0,3},{1,2},{2,1},{3,0},{4,7},{5,6},{6,5},{7,4},{8,11},{9,10},{10,... | collective-permute-start | bytes 393224 | tf_op jit(solution)/shard_map/ppermute | solution.py:23
  10.5 8.4 %collective-permute-start.11 = (bf16[128,512]{1,0:T(8,128)(2,1)S(1)}, bf16[128,512]{1,0:T(8,128)(2,1)S(1)}, u32[]{:S(2)}, u32[]{:S(2)}) collective-permute-start(bf16[128,512]{1,0:T(8,128)(2,1)S(1)} %get-tuple-element.30), channel_id=1, source_target_pairs={{0,1},{1,0},{2,3},{3,2},{4,5},{5,4},{6,7},{7,6},{8,9},{9,8},{10,11... | collective-permute-start | bytes 393224 | tf_op jit(solution)/shard_map/ppermute | solution.py:23
  15.1 5.0 %collective-permute-start.8 = (bf16[2,128,256]{2,1,0:T(8,128)(2,1)S(1)}, bf16[2,128,256]{2,1,0:T(8,128)(2,1)S(1)}, u32[]{:S(2)}, u32[]{:S(2)}) collective-permute-start(bf16[2,128,256]{2,1,0:T(8,128)(2,1)S(1)} %get-tuple-element.53), channel_id=1, source_target_pairs={{0,16},{8,24},{16,0},{24,8},{1,17},{9,25},{17,1},{25,9},{2,18},{10... | collective-permute-start | bytes 393224 | tf_op jit(solution)/shard_map/ppermute | solution.py:23
  18.9 7.1 %collective-permute-start.12 = (bf16[2,128,512]{2,1,0:T(8,128)(2,1)S(1)}, bf16[2,128,512]{2,1,0:T(8,128)(2,1)S(1)}, u32[]{:S(2)}, u32[]{:S(2)}) collective-permute-start(bf16[2,128,512]{2,1,0:T(8,128)(2,1)S(1)} %pad_maximum_fusion.5.refs_4_), channel_id=1, source_target_pairs={{0,8},{8,0},{16,24},{24,16},{1,9},{9,1},{17,25},{25,17},{2,10},{10... | collective-permute-start | bytes 786440 | tf_op jit(solution)/shard_map/ppermute | solution.py:23
  20.1 5.9 %collective-permute-start.9 = (bf16[2,2,128,256]{3,2,1,0:T(8,128)(2,1)S(1)}, bf16[2,2,128,256]{3,2,1,0:T(8,128)(2,1)S(1)}, u32[]{:S(2)}, u32[]{:S(2)}) collective-permute-start(bf16[2,2,128,256]{3,2,1,0:T(8,128)(2,1)S(1)} %pad_maximum_fusion.4.refs_0_.refs_1_), channel_id=1, source_target_pairs={{0,8},{8,0},{16,24},{24,16},{1,9},{9,1},{17,25},{25,17},{2,10},{10... | collective-permute-start | bytes 786440 | tf_op jit(solution)/shard_map/ppermute | solution.py:23
  20.2 8.4 %collective-permute-start.3 = (bf16[128,512]{1,0:T(8,128)(2,1)S(1)}, bf16[128,512]{1,0:T(8,128)(2,1)S(1)}, u32[]{:S(2)}, u32[]{:S(2)}) collective-permute-start(bf16[128,512]{1,0:T(8,128)(2,1)S(1)} %get-tuple-element.24), channel_id=1, source_target_pairs={{0,6},{1,7},{2,4},{3,5},{4,2},{5,3},{6,0},{7,1},{8,14},{9,15},{10,... | collective-permute-start | bytes 393224 | tf_op jit(solution)/shard_map/ppermute | solution.py:23
  22.9 11.5 %collective-permute-start.4 = (bf16[128,512]{1,0:T(8,128)(2,1)S(1)}, bf16[128,512]{1,0:T(8,128)(2,1)S(1)}, u32[]{:S(2)}, u32[]{:S(2)}) collective-permute-start(bf16[128,512]{1,0:T(8,128)(2,1)S(1)} %get-tuple-element.25), channel_id=1, source_target_pairs={{0,4},{1,5},{2,6},{3,7},{4,0},{5,1},{6,2},{7,3},{8,12},{9,13},{10,... | collective-permute-start | bytes 393224 | tf_op jit(solution)/shard_map/ppermute | solution.py:23
  22.9 11.5 %collective-permute-start.5 = (bf16[128,512]{1,0:T(8,128)(2,1)S(1)}, bf16[128,512]{1,0:T(8,128)(2,1)S(1)}, u32[]{:S(2)}, u32[]{:S(2)}) collective-permute-start(bf16[128,512]{1,0:T(8,128)(2,1)S(1)} %get-tuple-element.26), channel_id=1, source_target_pairs={{0,2},{1,3},{2,0},{3,1},{4,6},{5,7},{6,4},{7,5},{8,10},{9,11},{10,... | collective-permute-start | bytes 393224 | tf_op jit(solution)/shard_map/ppermute | solution.py:23
  26.0 37.7 %copy-start.4 = (bf16[512,128]{1,0:T(8,128)(2,1)S(1)}, bf16[512,128]{1,0:T(8,128)(2,1)}, u32[]{:S(2)}) copy-start(bf16[512,128]{1,0:T(8,128)(2,1)} %param.9) | copy-start | bytes 393220
  27.3 42.4 %copy-start = (bf16[1024,256]{1,0:T(8,128)(2,1)S(1)}, bf16[1024,256]{1,0:T(8,128)(2,1)}, u32[]{:S(2)}) copy-start(bf16[1024,256]{1,0:T(8,128)(2,1)} %constant.57.clone.dft_ref) | copy-start | bytes 1572868
  34.5 11.0 %collective-permute-start.13 = (bf16[3,128,512]{2,1,0:T(8,128)(2,1)S(1)}, bf16[3,128,512]{2,1,0:T(8,128)(2,1)S(1)}, u32[]{:S(2)}, u32[]{:S(2)}) collective-permute-start(bf16[3,128,512]{2,1,0:T(8,128)(2,1)S(1)} %pad_maximum_fusion.2), channel_id=1, source_target_pairs={{0,8},{8,0},{16,24},{24,16},{1,9},{9,1},{17,25},{25,17},{2,10},{10... | collective-permute-start | bytes 1179656 | tf_op jit(solution)/shard_map/ppermute | solution.py:23
  34.6 8.8 %collective-permute-start.1 = (bf16[2,512,128]{2,1,0:T(8,128)(2,1)S(1)}, bf16[2,512,128]{2,1,0:T(8,128)(2,1)S(1)}, u32[]{:S(2)}, u32[]{:S(2)}) collective-permute-start(bf16[2,512,128]{2,1,0:T(8,128)(2,1)S(1)} %pad_maximum_fusion.3.refs_0_), channel_id=1, source_target_pairs={{0,16},{8,24},{16,0},{24,8},{1,17},{9,25},{17,1},{25,9},{2,18},{10... | collective-permute-start | bytes 786440 | tf_op jit(solution)/shard_map/ppermute | solution.py:23
  36.2 31.7 %collective-permute-start = (bf16[2,512,128]{2,1,0:T(8,128)(2,1)S(1)}, bf16[2,512,128]{2,1,0:T(8,128)(2,1)S(1)}, u32[]{:S(2)}, u32[]{:S(2)}) collective-permute-start(bf16[2,512,128]{2,1,0:T(8,128)(2,1)S(1)} %pad_maximum_fusion.3.refs_0_), channel_id=1, source_target_pairs={{0,8},{8,0},{16,24},{24,16},{1,9},{9,1},{17,25},{25,17},{2,10},{10... | collective-permute-start | bytes 786440 | tf_op jit(solution)/shard_map/ppermute | solution.py:23
  43.4 26.3 %collective-permute-start.2 = (bf16[2,512,128]{2,1,0:T(8,128)(2,1)S(1)}, bf16[2,512,128]{2,1,0:T(8,128)(2,1)S(1)}, u32[]{:S(2)}, u32[]{:S(2)}) collective-permute-start(bf16[2,512,128]{2,1,0:T(8,128)(2,1)S(1)} %collective-permute-done.1.refs_2_), channel_id=1, source_target_pairs={{0,8},{8,0},{16,24},{24,16},{1,9},{9,1},{17,25},{25,17},{2,10},{10... | collective-permute-start | bytes 786440 | tf_op jit(solution)/shard_map/ppermute | solution.py:23
  43.4 9.2 %collective-permute-start.14 = (bf16[4,256,128]{2,1,0:T(8,128)(2,1)S(1)}, bf16[4,256,128]{2,1,0:T(8,128)(2,1)S(1)}, u32[]{:S(2)}, u32[]{:S(2)}) collective-permute-start(bf16[4,256,128]{2,1,0:T(8,128)(2,1)S(1)} %get-tuple-element.31), channel_id=1, source_target_pairs={{0,1},{1,0},{2,3},{3,2},{4,5},{5,4},{6,7},{7,6},{8,9},{9,8},{10,11... | collective-permute-start | bytes 786440 | tf_op jit(solution)/shard_map/ppermute | solution.py:23
  45.0 12.7 %collective-permute-start.18 = (bf16[4,256,128]{2,1,0:T(8,128)(2,1)S(1)}, bf16[4,256,128]{2,1,0:T(8,128)(2,1)S(1)}, u32[]{:S(2)}, u32[]{:S(2)}) collective-permute-start(bf16[4,256,128]{2,1,0:T(8,128)(2,1)S(1)} %get-tuple-element.39), channel_id=1, source_target_pairs={{0,1},{1,0},{2,3},{3,2},{4,5},{5,4},{6,7},{7,6},{8,9},{9,8},{10,11... | collective-permute-start | bytes 786440 | tf_op jit(solution)/shard_map/ppermute | solution.py:23
  52.6 6.1 %collective-permute-start.15 = (bf16[256,128]{1,0:T(8,128)(2,1)S(1)}, bf16[256,128]{1,0:T(8,128)(2,1)S(1)}, u32[]{:S(2)}, u32[]{:S(2)}) collective-permute-start(bf16[256,128]{1,0:T(8,128)(2,1)S(1)} %get-tuple-element.51), channel_id=1, source_target_pairs={{0,6},{1,7},{2,4},{3,5},{4,2},{5,3},{6,0},{7,1},{8,14},{9,15},{10,... | collective-permute-start | bytes 196616 | tf_op jit(solution)/shard_map/ppermute | solution.py:23
  55.3 6.1 %collective-permute-start.16 = (bf16[256,128]{1,0:T(8,128)(2,1)S(1)}, bf16[256,128]{1,0:T(8,128)(2,1)S(1)}, u32[]{:S(2)}, u32[]{:S(2)}) collective-permute-start(bf16[256,128]{1,0:T(8,128)(2,1)S(1)} %get-tuple-element.50), channel_id=1, source_target_pairs={{0,4},{1,5},{2,6},{3,7},{4,0},{5,1},{6,2},{7,3},{8,12},{9,13},{10,... | collective-permute-start | bytes 196616 | tf_op jit(solution)/shard_map/ppermute | solution.py:23
  57.7 4.4 %collective-permute-start.17 = (bf16[256,128]{1,0:T(8,128)(2,1)S(1)}, bf16[256,128]{1,0:T(8,128)(2,1)S(1)}, u32[]{:S(2)}, u32[]{:S(2)}) collective-permute-start(bf16[256,128]{1,0:T(8,128)(2,1)S(1)} %get-tuple-element.49), channel_id=1, source_target_pairs={{0,2},{1,3},{2,0},{3,1},{4,6},{5,7},{6,4},{7,5},{8,10},{9,11},{10,... | collective-permute-start | bytes 196616 | tf_op jit(solution)/shard_map/ppermute | solution.py:23
  58.7 6.7 %collective-permute-start.19 = (bf16[256,128]{1,0:T(8,128)(2,1)S(1)}, bf16[256,128]{1,0:T(8,128)(2,1)S(1)}, u32[]{:S(2)}, u32[]{:S(2)}) collective-permute-start(bf16[256,128]{1,0:T(8,128)(2,1)S(1)} %get-tuple-element.48), channel_id=1, source_target_pairs={{0,6},{1,7},{2,4},{3,5},{4,2},{5,3},{6,0},{7,1},{8,14},{9,15},{10,... | collective-permute-start | bytes 196616 | tf_op jit(solution)/shard_map/ppermute | solution.py:23
  61.4 5.9 %collective-permute-start.20 = (bf16[256,128]{1,0:T(8,128)(2,1)S(1)}, bf16[256,128]{1,0:T(8,128)(2,1)S(1)}, u32[]{:S(2)}, u32[]{:S(2)}) collective-permute-start(bf16[256,128]{1,0:T(8,128)(2,1)S(1)} %get-tuple-element.47), channel_id=1, source_target_pairs={{0,4},{1,5},{2,6},{3,7},{4,0},{5,1},{6,2},{7,3},{8,12},{9,13},{10,... | collective-permute-start | bytes 196616 | tf_op jit(solution)/shard_map/ppermute | solution.py:23
  62.1 5.4 %collective-permute-start.21 = (bf16[256,128]{1,0:T(8,128)(2,1)S(1)}, bf16[256,128]{1,0:T(8,128)(2,1)S(1)}, u32[]{:S(2)}, u32[]{:S(2)}) collective-permute-start(bf16[256,128]{1,0:T(8,128)(2,1)S(1)} %get-tuple-element.46), channel_id=1, source_target_pairs={{0,2},{1,3},{2,0},{3,1},{4,6},{5,7},{6,4},{7,5},{8,10},{9,11},{10,... | collective-permute-start | bytes 196616 | tf_op jit(solution)/shard_map/ppermute | solution.py:23
  65.4 4.3 %collective-permute-start.26 = (bf16[256,128]{1,0:T(8,128)(2,1)S(1)}, bf16[256,128]{1,0:T(8,128)(2,1)S(1)}, u32[]{:S(2)}, u32[]{:S(2)}) collective-permute-start(bf16[256,128]{1,0:T(8,128)(2,1)S(1)} %fusion.7.refs_0_), channel_id=1, source_target_pairs={{0,16},{8,24},{16,0},{24,8},{1,17},{9,25},{17,1},{25,9},{2,18},{10... | collective-permute-start | bytes 196616 | tf_op jit(solution)/shard_map/ppermute | solution.py:23
  67.3 4.9 %collective-permute-start.25 = (bf16[256,128]{1,0:T(8,128)(2,1)S(1)}, bf16[256,128]{1,0:T(8,128)(2,1)S(1)}, u32[]{:S(2)}, u32[]{:S(2)}) collective-permute-start(bf16[256,128]{1,0:T(8,128)(2,1)S(1)} %fusion.7.refs_0_), channel_id=1, source_target_pairs={{0,8},{8,0},{16,24},{24,16},{1,9},{9,1},{17,25},{25,17},{2,10},{10... | collective-permute-start | bytes 196616 | tf_op jit(solution)/shard_map/ppermute | solution.py:23
  67.5 6.0 %collective-permute-start.24 = (bf16[256,128]{1,0:T(8,128)(2,1)S(1)}, bf16[256,128]{1,0:T(8,128)(2,1)S(1)}, u32[]{:S(2)}, u32[]{:S(2)}) collective-permute-start(bf16[256,128]{1,0:T(8,128)(2,1)S(1)} %fusion.3.refs_0_), channel_id=1, source_target_pairs={{0,8},{8,0},{16,24},{24,16},{1,9},{9,1},{17,25},{25,17},{2,10},{10... | collective-permute-start | bytes 196616 | tf_op jit(solution)/shard_map/ppermute | solution.py:23
  67.9 4.3 %collective-permute-start.22 = (bf16[256,128]{1,0:T(8,128)(2,1)S(1)}, bf16[256,128]{1,0:T(8,128)(2,1)S(1)}, u32[]{:S(2)}, u32[]{:S(2)}) collective-permute-start(bf16[256,128]{1,0:T(8,128)(2,1)S(1)} %fusion.3.refs_0_), channel_id=1, source_target_pairs={{0,16},{8,24},{16,0},{24,8},{1,17},{9,25},{17,1},{25,9},{2,18},{10... | collective-permute-start | bytes 196616 | tf_op jit(solution)/shard_map/ppermute | solution.py:23
  69.6 2.5 %collective-permute-start.27 = (bf16[256,128]{1,0:T(8,128)(2,1)S(1)}, bf16[256,128]{1,0:T(8,128)(2,1)S(1)}, u32[]{:S(2)}, u32[]{:S(2)}) collective-permute-start(bf16[256,128]{1,0:T(8,128)(2,1)S(1)} %collective-permute-done.26.refs_2_), channel_id=1, source_target_pairs={{0,8},{8,0},{16,24},{24,16},{1,9},{9,1},{17,25},{25,17},{2,10},{10... | collective-permute-start | bytes 196616 | tf_op jit(solution)/shard_map/ppermute | solution.py:23
  72.2 2.0 %collective-permute-start.23 = (bf16[256,128]{1,0:T(8,128)(2,1)S(1)}, bf16[256,128]{1,0:T(8,128)(2,1)S(1)}, u32[]{:S(2)}, u32[]{:S(2)}) collective-permute-start(bf16[256,128]{1,0:T(8,128)(2,1)S(1)} %collective-permute-done.22.refs_0_), channel_id=1, source_target_pairs={{0,8},{8,0},{16,24},{24,16},{1,9},{9,1},{17,25},{25,17},{2,10},{10... | collective-permute-start | bytes 196616 | tf_op jit(solution)/shard_map/ppermute | solution.py:23
  (1 other events, 1.0 us)
where the time goes:
time: 76.6 us; the launch traced here: 76.4 us
  waiting for transfers between devices  34.6 us (45%)
  starting transfers between devices  28.5 us (37%)
  Pallas kernels  11.2 us (15%)
  between operations  0.92 us (1%)
    ppermute x28, waiting for transfers between devices, swapped(): return lax.ppermute(block, axis, [(i, i ^ mask) for i in range(size)])  34.6 us
    ppermute x28, starting transfers between devices, swapped(): return lax.ppermute(block, axis, [(i, i ^ mask) for i in range(size)])  28.5 us
    pallas_call x3, Pallas kernels, add_blocks(): pl.pallas_call(functools.partial(add_kernel, offsets, which, first, last)...  3.79 us
    pallas_call x2, Pallas kernels, product(): pl.pallas_call(functools.partial(product_kernel, sizes), out_shape=(jax.S...  2.58 us
    pallas_call x1, Pallas kernels, prepare(): pl.pallas_call(functools.partial(prepare_kernel, widths), out_shape=[jax....  1.92 us
    pallas_call x1, Pallas kernels, lag_spectra(): pl.pallas_call(functools.partial(lag_kernel, n), out_shape=jax.ShapeDtype...  1.69 us
  transfers between devices with their start and end apart: 28, of which 16 were waited for; matrix products, arithmetic and copies ran while one was open for 1% of the time, Pallas kernels for 10%

commit v1 on v0

v1 whole, which is shorter than its diff:
```python
import functools
import math

import jax
import jax.numpy as jnp
import numpy as np
from jax import lax
from jax.experimental import pallas as pl
from jax.experimental.pallas import tpu as pltpu
from jax.sharding import PartitionSpec as P


SUB = 256
LANES = 128
VMEM = pl.BlockSpec(memory_space=pltpu.VMEM)
F32, BF16 = jnp.float32, jnp.bfloat16
NT = (((1,), (1,)), ((), ()))


def swapped(block, axis, mask):
    size = lax.axis_size(axis)
    return lax.ppermute(block, axis, [(i, i ^ mask) for i in range(size)])


def dft_parts():
    freq = np.arange(SUB)[:, None]
    place = np.arange(SUB)[None, :]
    angle = (((2 * freq + 1) * place) % (4 * SUB)).astype(np.float64) * (math.pi / (2 * SUB))
    matrix = np.concatenate([np.cos(angle), -np.sin(angle)], axis=0).astype(np.float32)
    upper = matrix.astype(jnp.bfloat16)
    lower = (matrix - upper.astype(np.float32)).astype(jnp.bfloat16)
    return np.concatenate([upper, lower], axis=0), np.concatenate([upper.T, lower.T], axis=0)


def dot(a, b):
    return jnp.dot(a, b, preferred_element_type=F32)


def dot_parts(parts_ref, b):
    both = dot(parts_ref[...], b)
    half = both.shape[0] // 2
    return both[:half] + both[half:]


def prepare_kernel(features, wanted, w_ref, *refs):
    outs, sems = refs[:-1], refs[-1]
    chan = lax.axis_index("chan")
    copies = []
    for i, (mask, split, other_core) in enumerate(wanted):
        width = outs[i].shape[-1]
        start = (chan ^ mask) * features + start_of(features, split, other_core, 0)
        source = w_ref.at[:, pl.ds(pl.multiple_of(start, width), width)]
        copies.append(pltpu.make_async_copy(source, outs[i], sems.at[i]))
    for copy in copies:
        copy.start()
    for copy in copies:
        copy.wait()


def prepare(w_out, features, wanted):
    rows = w_out.shape[0]
    widths = [features // (4 if split else 2) for _, split, _ in wanted]
    return pl.pallas_call(
        functools.partial(prepare_kernel, features, wanted),
        out_shape=[jax.ShapeDtypeStruct((rows, width), w_out.dtype) for width in widths],
        in_specs=[pl.BlockSpec(memory_space=pltpu.HBM)],
        out_specs=[VMEM] * len(widths),
        scratch_shapes=[pltpu.SemaphoreType.DMA((len(widths),))],
        compiler_params=pltpu.CompilerParams(vmem_limit_bytes=GRANT[0] << 20),
        cost_estimate=pl.CostEstimate(flops=0, bytes_accessed=4 << 20, transcendentals=0),
    )(w_out)


PIECES = 4


def hold_kernel(source_ref, out_ref, sems):
    rows = source_ref.shape[0] // PIECES
    copies = [
        pltpu.make_async_copy(source_ref.at[pl.ds(i * rows, rows)], out_ref.at[pl.ds(i * rows, rows)], sems.at[i])
        for i in range(PIECES)
    ]
    for copy in copies:
        copy.start()
    for copy in copies:
        copy.wait()


def hold(block):
    return pl.pallas_call(
        hold_kernel,
        out_shape=jax.ShapeDtypeStruct(block.shape, block.dtype),
        in_specs=[pl.BlockSpec(memory_space=pltpu.HBM)],
        out_specs=VMEM,
        scratch_shapes=[pltpu.SemaphoreType.DMA((PIECES,))],
        compiler_params=pltpu.CompilerParams(vmem_limit_bytes=GRANT[1] << 20),
        cost_estimate=pl.CostEstimate(flops=0, bytes_accessed=2 << 20, transcendentals=0),
    )(block)


def start_of(features, split, other_core, other_side):
    seq = lax.axis_index("seq")
    core, side = (seq & 1) ^ other_core, ((seq >> 1) & 1) ^ other_side
    return core * (features // 2) + (side * (features // 4) if split else 0)


def product_kernel(sizes, d_ref, *refs):
    parts, outs = refs[: len(sizes)], refs[len(sizes) :]
    count = outs[0].shape[0]
    channels = outs[0].shape[-1]
    for which in range(2):
        rows = pl.ds(which * SUB, SUB)
        lefts = []
        for part, (_, _, _, whose) in zip(parts, sizes):
            width = part.shape[-1]
            start = pl.multiple_of(start_of(d_ref.shape[1], *whose), width)
            lefts.append(d_ref[rows, pl.ds(start, width)])
        for i in range(0, count, 2):
            total = None
            for left, part, (index, first, masks, _) in zip(lefts, parts, sizes):
                if not first <= i < first + masks:
                    continue
                w = jnp.concatenate([part[(*index, i - first)], part[(*index, i + 1 - first)]], axis=0)
                term = lax.dot_general(left, w, NT, preferred_element_type=F32)
                total = term if total is None else total + term
            outs[which][i] = total[:, :channels].astype(outs[which].dtype)
            outs[which][i + 1] = total[:, channels:].astype(outs[which].dtype)


def product(d_out, parts, out_type):
    count = max(first + block.shape[-3] for block, _, first, _ in parts)
    channels = parts[0][0].shape[-2]
    sizes = [(index, first, block.shape[-3], whose) for block, index, first, whose in parts]
    return pl.pallas_call(
        functools.partial(product_kernel, sizes),
        out_shape=(jax.ShapeDtypeStruct((count, SUB, channels), out_type),) * 2,
        in_specs=[VMEM] * (1 + len(parts)),
        out_specs=(VMEM, VMEM),
        compiler_params=pltpu.CompilerParams(vmem_limit_bytes=8 << 20),
        cost_estimate=pl.CostEstimate(
            flops=4 * count * SUB * channels * d_out.shape[1], bytes_accessed=4 << 20, transcendentals=0
        ),
    )(d_out, *[block for block, _, _, _ in parts])


def lag_kernel(n, dft_ref, *refs):
    blocks, out_ref, spec = refs[:n], refs[n], refs[n + 1]
    me = lax.axis_index("seq")
    spec[0] = jnp.zeros_like(spec[0])
    out_ref[0] = jnp.zeros_like(out_ref[0])
    for offset in range(n):
        place = (me ^ offset) * 2 + 1
        for sub in range(2):
            rows = pl.ds(sub * SUB, SUB)
            data = jnp.concatenate([blocks[offset][0, rows, :], blocks[offset][1, rows, :]], axis=1)
            both = dot_parts(dft_ref, data)
            channels = data.shape[1] // 2
            spec[place + sub, 0] = both[:, :channels] * (1.0 / SUB)
            spec[place + sub, 1] = both[:, channels:] * (1.0 / SUB)
    channels = spec.shape[-1]
    sign = (1 - 2 * (lax.broadcasted_iota(jnp.int32, (SUB, channels), 0) % 2)).astype(F32)

    @pl.loop(0, 2 * n)
    def _(lag):
        for which in range(2):
            out_ref[lag + 1, which, :SUB] = spec[lag + 1, which, :SUB] - sign * spec[lag, which, SUB:]
            out_ref[lag + 1, which, SUB:] = spec[lag + 1, which, SUB:] + sign * spec[lag, which, :SUB]


def lag_spectra(dft, blocks):
    n = len(blocks)
    channels = blocks[0].shape[-1]
    return pl.pallas_call(
        functools.partial(lag_kernel, n),
        out_shape=jax.ShapeDtypeStruct((2 * n + 1, 2, 2 * SUB, channels), F32),
        in_specs=[VMEM] * (1 + n),
        out_specs=VMEM,
        scratch_shapes=[pltpu.VMEM((2 * n + 1, 2, 2 * SUB, channels), F32)],
        compiler_params=pltpu.CompilerParams(vmem_limit_bytes=(4 + 3 * n) << 20),
        cost_estimate=pl.CostEstimate(
            flops=16 * n * SUB * SUB * channels * 2, bytes_accessed=6 << 20, transcendentals=0
        ),
    )(dft, *blocks)


CHUNK = 32
GRANT = (51, 52)


def add_kernel(offsets, which, first, last, dft_ref, lag_ref, *refs):
    blocks, refs = refs[: len(offsets)], list(refs[len(offsets) :])
    before = None if first else refs.pop(0)
    if last:
        back_ref, inner_ref, filter_ref, spec, total = refs
    else:
        total, spec = refs
    me = lax.axis_index("seq")
    channels = spec.shape[-1]
    for pair in range(0, len(offsets), 2):
        used = offsets[pair : pair + 2]
        data = jnp.concatenate([blocks[pair + i][...] for i in range(len(used))], axis=1)
        both = dot_parts(dft_ref, data)
        for i in range(len(used)):
            spec[pair + i] = both[:, i * channels : (i + 1) * channels]

    for array in range(2):
        for chunk in range(SUB // CHUNK):
            real, imag = pl.ds(chunk * CHUNK, CHUNK), pl.ds(SUB + chunk * CHUNK, CHUNK)
            places = [slice((2 * array + sub) * channels, (2 * array + sub + 1) * channels) for sub in range(2)]
            zero = jnp.zeros((CHUNK, channels), F32)
            sums = [(zero, zero) if first else (before[real, p], before[imag, p]) for p in places]
            for place, offset in enumerate(offsets):
                step = (me ^ offset) - me
                g_real, g_imag = spec[place, real, :], spec[place, imag, :]
                for sub in range(2):
                    lag = jnp.maximum(step * 2 + which - sub + 1, 0)
                    k_real, k_imag = lag_ref[lag, array, real, :], lag_ref[lag, array, imag, :]
                    s_real, s_imag = sums[sub]
                    s_real = s_real + g_real * k_real + g_imag * k_imag
                    s_imag = s_imag + g_imag * k_real - g_real * k_imag
                    sums[sub] = (s_real, s_imag)
            for p, (s_real, s_imag) in zip(places, sums):
                total[real, p] = s_real
                total[imag, p] = s_imag
        if not last:
            continue
        whole = total[:, 2 * array * channels : 2 * (array + 1) * channels]
        high = whole.astype(BF16)
        low = (whole - high.astype(F32)).astype(BF16)
        values = dot_parts(back_ref, high) + dot(back_ref[:SUB, :], low)
        out_ref = (inner_ref, filter_ref)[array]
        out_ref[:SUB, :] = values[:, :channels].astype(out_ref.dtype)
        out_ref[SUB:, :] = values[:, channels:].astype(out_ref.dtype)


def add_blocks(n, dft, lags, blocks, which, before=None, back=None):
    offsets = sorted(blocks)
    blocks = [blocks[offset] for offset in offsets]
    channels = blocks[0].shape[-1]
    first, last = before is None, back is not None
    whole = jax.ShapeDtypeStruct((2 * SUB, 4 * channels), F32)
    out_shape = whole
    scratch = [pltpu.VMEM((len(blocks), 2 * SUB, channels), F32)]
    if last:
        out_shape = (
            jax.ShapeDtypeStruct((2 * SUB, channels), BF16),
            jax.ShapeDtypeStruct((2 * SUB, channels), F32),
        )
        scratch.append(pltpu.VMEM(whole.shape, F32))
    args = (dft, lags, *blocks) + (() if first else (before,)) + ((back,) if last else ())
    return pl.pallas_call(
        functools.partial(add_kernel, offsets, which, first, last),
        out_shape=out_shape,
        in_specs=[VMEM] * len(args),
        out_specs=(VMEM, VMEM) if last else VMEM,
        scratch_shapes=scratch,
        compiler_params=pltpu.CompilerParams(vmem_limit_bytes=(6 + 2 * n) << 20),
        cost_estimate=pl.CostEstimate(
            flops=8 * len(blocks) * SUB * SUB * channels * 2, bytes_accessed=4 << 20, transcendentals=0
        ),
    )(*args)


def spread_offsets(size):
    if size <= 4:
        return [(offset, 0, offset) for offset in reversed(range(1, size))]
    held, moves, mask = [0], [], size // 2
    while mask:
        new = [(offset | mask, offset, mask) for offset in held]
        moves += new
        held += [offset for offset, _, _ in new]
        mask //= 2
    return moves


def spread_blocks(block, axis):
    size = lax.axis_size(axis)
    held = {0: block}
    for offset, source, mask in spread_offsets(size):
        held[offset] = swapped(held[source], axis, mask)
    return held


def masks_of(chan_n):
    odd = [m for m in reversed(range(chan_n)) if m % 2]
    return odd, [m - 1 for m in odd]


def far_count(chan_n, features):
    return chan_n // 4 if features % (4 * LANES) == 0 else 0


def body(d_out, w_out, gate, inner, filt):
    chan_n = lax.axis_size("chan")
    features = d_out.shape[1]
    odd, even = masks_of(chan_n)
    groups = chan_n // 2
    far = far_count(chan_n, features)

    wanted = [(mask, i < far, 0) for i, mask in enumerate(odd)] + [(mask, False, 0) for mask in even] + [(0, False, 1)]
    blocks = list(prepare(w_out, features, wanted))
    d_out = hold(d_out)
    for i, mask in enumerate(odd + even[:-1]):
        blocks[i] = swapped(blocks[i], "chan", mask)
    odd_parts, even_parts = [], []
    if far:
        sides = [swapped(blocks[i], "seq", 2) for i in range(far)]
        owns = [jnp.stack([blocks[i], sides[i]]) for i in range(far)]
        twins = [swapped(owns[i], "seq", 1) for i in range(far)]
        for other_core, block in enumerate((jnp.stack(owns, axis=1), jnp.stack(twins, axis=1))):
            for other_side in range(2):
                odd_parts.append((block, (other_side,), 0, (True, other_core, other_side)))
    near = jnp.stack(blocks[far:groups])
    twin = swapped(near, "seq", 1)
    odd_parts += [(near, (), far, (False, 0, 0)), (twin, (), far, (False, 1, 0))]
    lag_pair = jnp.stack([filt, inner])
    lag_blocks = [block for _, block in sorted(spread_blocks(lag_pair, "seq").items())]
    dft, back = dft_parts()

    p_odd = product(d_out, odd_parts, BF16)
    *later, _ = lax.optimization_barrier((*blocks[groups : 2 * groups - 1], p_odd[0]))
    near = jnp.stack(later)
    twin = swapped(near, "seq", 1)
    even_parts = [
        (jnp.concatenate([near, blocks[-2][None]]), (), 0, (False, 0, 0)),
        (jnp.concatenate([twin, blocks[-1][None]]), (), 0, (False, 1, 0)),
    ]
    from_pair = [swapped(p_odd[which], "chan", 1) for which in range(2)]
    lags = lag_spectra(dft, lag_blocks)
    p_even = product(d_out, even_parts, F32)
    own, parts = [], []
    for which in range(2):
        mine, theirs = p_even[which], from_pair[which]
        sent = []
        for i, mask in enumerate(even):
            if which and i == groups - 2:
                mine, theirs, *_ = lax.optimization_barrier((mine, theirs, *sent))
            total = mine[i] + theirs[i].astype(F32)
            sent.append(total.astype(BF16) if mask else total)
        own.append(sent.pop())
        parts.append([swapped(block, "chan", mask) for block, mask in zip(sent, even)])
    grad_blocks = []
    for which in range(2):
        grad_gated = own[which]
        for part in parts[which]:
            grad_gated = grad_gated + part.astype(F32)
        gate_part = gate[which * SUB : (which + 1) * SUB].astype(F32)
        grad_conv = (gate_part * grad_gated).astype(BF16)
        gate, grad_conv = lax.optimization_barrier((gate, grad_conv))
        grad_blocks.append(spread_blocks(grad_conv, "seq"))
    seq_n = lax.axis_size("seq")
    groups_of = stages(seq_n)
    total = None
    for i, (which, offsets) in enumerate(groups_of):
        last = i == len(groups_of) - 1
        chosen = {offset: grad_blocks[which][offset] for offset in offsets}
        total = add_blocks(seq_n, dft, lags, chosen, which, total, back if last else None)
    return tuple(total)


def stages(seq_n):
    near = [0, 1] if seq_n > 1 else [0]
    rest = [offset for offset in range(seq_n) if offset not in near]
    return [(0, list(range(seq_n))), (1, near)] + ([(1, rest)] if rest else [])


def solution(mesh):
    placed = (
        P("seq", "chan"),
        P("chan", None),
        P("seq", "chan"),
        P("seq", "chan"),
        P("seq", "chan"),
    )

    return jax.shard_map(
        body,
        mesh=mesh,
        in_specs=placed,
        out_specs=(P("seq", "chan"), P("seq", "chan")),
        check_vma=False,
    )
```

time: 76.6 us -> 75.3 us (0.983)
  starting transfers between devices: 28.5 us -> 31.5 us
  Pallas kernels: 11.2 us -> 9.38 us
  waiting for transfers between devices: 34.6 us -> 32.8 us
    ppermute x28 -> x30, starting transfers between devices: 28.5 us -> 31.5 us  [swapped(): return lax.ppermute(block, axis, [(i, i ^ mask) for i in range(size)])]
    ppermute x28 -> x30, waiting for transfers between devices: 34.6 us -> 32.8 us  [swapped(): return lax.ppermute(block, axis, [(i, i ^ mask) for i in range(size)])]
    pallas_call x2, Pallas kernels: 2.58 us -> 1.51 us  [product(): pl.pallas_call(functools.partial(product_kernel, sizes), out_shape=(jax.S...]
  transfers between devices with their start and end apart: 28 -> 30, of which waited for: 16 -> 14; matrix products, arithmetic and copies ran while one was open for 1% -> 1% of each run, Pallas kernels for 10% -> 8%
where the time goes in v1:
time: 75.3 us; the launch traced here: 75.2 us
  waiting for transfers between devices  32.8 us (44%)
  starting transfers between devices  31.5 us (42%)
  Pallas kernels  9.38 us (12%)
  between operations  0.91 us (1%)
    ppermute x30, waiting for transfers between devices, swapped(): return lax.ppermute(block, axis, [(i, i ^ mask) for i in range(size)])  32.8 us
    ppermute x30, starting transfers between devices, swapped(): return lax.ppermute(block, axis, [(i, i ^ mask) for i in range(size)])  31.5 us
    pallas_call x3, Pallas kernels, add_blocks(): pl.pallas_call(functools.partial(add_kernel, offsets, which, first, last)...  3.57 us
    pallas_call x1, Pallas kernels, lag_spectra(): pl.pallas_call(functools.partial(lag_kernel, n), out_shape=jax.ShapeDtype...  1.69 us
    pallas_call x2, Pallas kernels, product(): pl.pallas_call(functools.partial(product_kernel, sizes), out_shape=(jax.S...  1.51 us
  transfers between devices with their start and end apart: 30, of which 14 were waited for; matrix products, arithmetic and copies ran while one was open for 1% of the time, Pallas kernels for 8%

profile of v1, /device:TPU:0, one launch (start us, length us, event | category | flops | bytes accessed | tf_op | source)
XLA Modules:
  0.0 75.2 jit_solution(6987150362469438251)
XLA Ops:
  0.6 1.4 %shard_map.88 = (bf16[128,256]{1,0:T(8,128)(2,1)S(1)}, bf16[128,256]{1,0:T(8,128)(2,1)S(1)}, bf16[128,512]{1,0:T(8,128)(2,1)S(1)}, bf16[128,512]{1,0:T(8,128)(2,...) custom-call(bf16[128,8192]{1,0:T(8,128)(2,1)} %w_ref.1), custom_call_target="tpu_custom_call" | custom-call | bytes 4194304 | tf_op jit(solution)/shard_map/pallas_call | solution.py:63
  2.0 5.1 %collective-permute-start.8 = (bf16[128,256]{1,0:T(8,128)(2,1)S(1)}, bf16[128,256]{1,0:T(8,128)(2,1)S(1)}, u32[]{:S(2)}, u32[]{:S(2)}) collective-permute-start(bf16[128,256]{1,0:T(8,128)(2,1)S(1)} %get-tuple-element.27), channel_id=1, source_target_pairs={{0,5},{1,4},{2,7},{3,6},{4,1},{5,0},{6,3},{7,2},{8,13},{9,12},{10,... | collective-permute-start | bytes 196616 | tf_op jit(solution)/shard_map/ppermute | solution.py:22
  7.1 1.3 %collective-permute-start.6 = (bf16[128,256]{1,0:T(8,128)(2,1)S(1)}, bf16[128,256]{1,0:T(8,128)(2,1)S(1)}, u32[]{:S(2)}, u32[]{:S(2)}) collective-permute-start(bf16[128,256]{1,0:T(8,128)(2,1)S(1)} %get-tuple-element.26), channel_id=1, source_target_pairs={{0,7},{1,6},{2,5},{3,4},{4,3},{5,2},{6,1},{7,0},{8,15},{9,14},{10,... | collective-permute-start | bytes 196616 | tf_op jit(solution)/shard_map/ppermute | solution.py:22
  8.4 2.4 %collective-permute-done.8 = bf16[128,256]{1,0:T(8,128)(2,1)S(1)} collective-permute-done((bf16[128,256]{1,0:T(8,128)(2,1)S(1)}, bf16[128,256]{1,0:T(8,128)(2,1)S(1)}, u32[]{:S(2)}, u32[]{:S(2)}) %collective-permute-start.8) | collective-permute-done | bytes 65568 | tf_op jit(solution)/shard_map/ppermute | solution.py:22
  10.8 1.6 %collective-permute-start.9 = (bf16[128,256]{1,0:T(8,128)(2,1)S(1)}, bf16[128,256]{1,0:T(8,128)(2,1)S(1)}, u32[]{:S(2)}, u32[]{:S(2)}) collective-permute-start(bf16[128,256]{1,0:T(8,128)(2,1)S(1)} %collective-permute-done.8), channel_id=1, source_target_pairs={{0,16},{8,24},{16,0},{24,8},{1,17},{9,25},{17,1},{25,9},{2,18},{10... | collective-permute-start | bytes 196616 | tf_op jit(solution)/shard_map/ppermute | solution.py:22
  12.4 2.0 %collective-permute-start.12 = (bf16[128,512]{1,0:T(8,128)(2,1)S(1)}, bf16[128,512]{1,0:T(8,128)(2,1)S(1)}, u32[]{:S(2)}, u32[]{:S(2)}) collective-permute-start(bf16[128,512]{1,0:T(8,128)(2,1)S(1)} %get-tuple-element.28), channel_id=1, source_target_pairs={{0,3},{1,2},{2,1},{3,0},{4,7},{5,6},{6,5},{7,4},{8,11},{9,10},{10,... | collective-permute-start | bytes 393224 | tf_op jit(solution)/shard_map/ppermute | solution.py:22
  14.5 1.6 %collective-permute-start.13 = (bf16[128,512]{1,0:T(8,128)(2,1)S(1)}, bf16[128,512]{1,0:T(8,128)(2,1)S(1)}, u32[]{:S(2)}, u32[]{:S(2)}) collective-permute-start(bf16[128,512]{1,0:T(8,128)(2,1)S(1)} %get-tuple-element.29), channel_id=1, source_target_pairs={{0,1},{1,0},{2,3},{3,2},{4,5},{5,4},{6,7},{7,6},{8,9},{9,8},{10,11... | collective-permute-start | bytes 393224 | tf_op jit(solution)/shard_map/ppermute | solution.py:22
  16.7 1.7 %collective-permute-done.12 = bf16[128,512]{1,0:T(8,128)(2,1)S(1)} collective-permute-done((bf16[128,512]{1,0:T(8,128)(2,1)S(1)}, bf16[128,512]{1,0:T(8,128)(2,1)S(1)}, u32[]{:S(2)}, u32[]{:S(2)}) %collective-permute-start.12) | collective-permute-done | bytes 131104 | tf_op jit(solution)/shard_map/ppermute | solution.py:22
  18.4 1.4 %collective-permute-done.13 = bf16[128,512]{1,0:T(8,128)(2,1)S(1)} collective-permute-done((bf16[128,512]{1,0:T(8,128)(2,1)S(1)}, bf16[128,512]{1,0:T(8,128)(2,1)S(1)}, u32[]{:S(2)}, u32[]{:S(2)}) %collective-permute-start.13) | collective-permute-done | bytes 131104 | tf_op jit(solution)/shard_map/ppermute | solution.py:22
  20.5 4.6 %collective-permute-start.3 = (bf16[128,512]{1,0:T(8,128)(2,1)S(1)}, bf16[128,512]{1,0:T(8,128)(2,1)S(1)}, u32[]{:S(2)}, u32[]{:S(2)}) collective-permute-start(bf16[128,512]{1,0:T(8,128)(2,1)S(1)} %get-tuple-element.23), channel_id=1, source_target_pairs={{0,6},{1,7},{2,4},{3,5},{4,2},{5,3},{6,0},{7,1},{8,14},{9,15},{10,... | collective-permute-start | bytes 393224 | tf_op jit(solution)/shard_map/ppermute | solution.py:22
  25.2 1.2 %shard_map.87.d_ref = bf16[512,1024]{1,0:T(8,128)(2,1)S(1)} custom-call(bf16[512,1024]{1,0:T(8,128)(2,1)} %source_ref.1), custom_call_target="tpu_custom_call" | custom-call | bytes 2097152 | tf_op jit(solution)/shard_map/pallas_call | solution.py:90
  27.2 0.8 %shard_map.89 = (bf16[4,256,128]{2,1,0:T(8,128)(2,1)S(1)}, bf16[4,256,128]{2,1,0:T(8,128)(2,1)S(1)}) custom-call(bf16[512,1024]{1,0:T(8,128)(2,1)S(1)} %shard_map.87.d_ref, bf16[2,2,128,256]{3,2,1,0:T(8,128)(2,1)S(1)} %copy.10.refs_0_.refs_1_, bf16[2,2,128,256]{3,2,1,0:T(8,128)(2,1)S(1)} %copy.10.refs_0_.refs_1_, ...), custom_call_target="tpu_custom_call" | custom-call | flops 536870912 | bytes 4194304 | tf_op jit(solution)/shard_map/pallas_call | solution.py:134
  28.0 1.4 %collective-permute-done.3 = bf16[128,512]{1,0:T(8,128)(2,1)S(1)} collective-permute-done((bf16[128,512]{1,0:T(8,128)(2,1)S(1)}, bf16[128,512]{1,0:T(8,128)(2,1)S(1)}, u32[]{:S(2)}, u32[]{:S(2)}) %collective-permute-start.3) | collective-permute-done | bytes 131104 | tf_op jit(solution)/shard_map/ppermute | solution.py:22
  29.4 7.9 %collective-permute-done.4 = bf16[128,512]{1,0:T(8,128)(2,1)S(1)} collective-permute-done((bf16[128,512]{1,0:T(8,128)(2,1)S(1)}, bf16[128,512]{1,0:T(8,128)(2,1)S(1)}, u32[]{:S(2)}, u32[]{:S(2)}) %collective-permute-start.4) | collective-permute-done | bytes 131104 | tf_op jit(solution)/shard_map/ppermute | solution.py:22
  38.1 1.4 %collective-permute-start.20 = (bf16[4,256,128]{2,1,0:T(8,128)(2,1)S(1)}, bf16[4,256,128]{2,1,0:T(8,128)(2,1)S(1)}, u32[]{:S(2)}, u32[]{:S(2)}) collective-permute-start(bf16[4,256,128]{2,1,0:T(8,128)(2,1)S(1)} %get-tuple-element.39), channel_id=1, source_target_pairs={{0,1},{1,0},{2,3},{3,2},{4,5},{5,4},{6,7},{7,6},{8,9},{9,8},{10,11... | collective-permute-start | bytes 786440 | tf_op jit(solution)/shard_map/ppermute | solution.py:22
  39.7 0.8 %shard_map.90 = (f32[4,256,128]{2,1,0:T(8,128)S(1)}, f32[4,256,128]{2,1,0:T(8,128)S(1)}) custom-call(bf16[512,1024]{1,0:T(8,128)(2,1)S(1)} %shard_map.87.d_ref, bf16[4,128,512]{2,1,0:T(8,128)(2,1)S(1)} %pad_maximum_fusion.refs_0_, bf16[4,128,512]{2,1,0:T(8,128)(2,1)S(1)} %pad_maximum_fusion.1.refs_1_), custom_call_target="tpu_custom_call" | custom-call | flops 536870912 | bytes 4194304 | tf_op jit(solution)/shard_map/pallas_call | solution.py:134
  40.4 6.2 %collective-permute-done.16 = bf16[4,256,128]{2,1,0:T(8,128)(2,1)S(1)} collective-permute-done((bf16[4,256,128]{2,1,0:T(8,128)(2,1)S(1)}, bf16[4,256,128]{2,1,0:T(8,128)(2,1)S(1)}, u32[]{:S(2)}, u32[]{:S(2)}) %collective-permute-start.16) | collective-permute-done | bytes 262176 | tf_op jit(solution)/shard_map/ppermute | solution.py:22
  46.7 2.8 %collective-permute-start.17 = (bf16[256,128]{1,0:T(8,128)(2,1)S(1)}, bf16[256,128]{1,0:T(8,128)(2,1)S(1)}, u32[]{:S(2)}, u32[]{:S(2)}) collective-permute-start(bf16[256,128]{1,0:T(8,128)(2,1)S(1)} %get-tuple-element.46), channel_id=1, source_target_pairs={{0,6},{1,7},{2,4},{3,5},{4,2},{5,3},{6,0},{7,1},{8,14},{9,15},{10,... | collective-permute-start | bytes 196616 | tf_op jit(solution)/shard_map/ppermute | solution.py:22
  49.5 1.7 %collective-permute-start.19 = (bf16[256,128]{1,0:T(8,128)(2,1)S(1)}, bf16[256,128]{1,0:T(8,128)(2,1)S(1)}, u32[]{:S(2)}, u32[]{:S(2)}) collective-permute-start(bf16[256,128]{1,0:T(8,128)(2,1)S(1)} %get-tuple-element.47), channel_id=1, source_target_pairs={{0,2},{1,3},{2,0},{3,1},{4,6},{5,7},{6,4},{7,5},{8,10},{9,11},{10,... | collective-permute-start | bytes 196616 | tf_op jit(solution)/shard_map/ppermute | solution.py:22
  52.0 0.8 %collective-permute-done.17 = bf16[256,128]{1,0:T(8,128)(2,1)S(1)} collective-permute-done((bf16[256,128]{1,0:T(8,128)(2,1)S(1)}, bf16[256,128]{1,0:T(8,128)(2,1)S(1)}, u32[]{:S(2)}, u32[]{:S(2)}) %collective-permute-start.17) | collective-permute-done | bytes 65568 | tf_op jit(solution)/shard_map/ppermute | solution.py:22
  53.4 1.5 %collective-permute-done.18 = bf16[256,128]{1,0:T(8,128)(2,1)S(1)} collective-permute-done((bf16[256,128]{1,0:T(8,128)(2,1)S(1)}, bf16[256,128]{1,0:T(8,128)(2,1)S(1)}, u32[]{:S(2)}, u32[]{:S(2)}) %collective-permute-start.18) | collective-permute-done | bytes 65568 | tf_op jit(solution)/shard_map/ppermute | solution.py:22
  54.9 2.2 %collective-permute-start.21 = (bf16[256,128]{1,0:T(8,128)(2,1)S(1)}, bf16[256,128]{1,0:T(8,128)(2,1)S(1)}, u32[]{:S(2)}, u32[]{:S(2)}) collective-permute-start(bf16[256,128]{1,0:T(8,128)(2,1)S(1)} %get-tuple-element.45), channel_id=1, source_target_pairs={{0,6},{1,7},{2,4},{3,5},{4,2},{5,3},{6,0},{7,1},{8,14},{9,15},{10,... | collective-permute-start | bytes 196616 | tf_op jit(solution)/shard_map/ppermute | solution.py:22
  57.7 4.0 %collective-permute-done.21 = bf16[256,128]{1,0:T(8,128)(2,1)S(1)} collective-permute-done((bf16[256,128]{1,0:T(8,128)(2,1)S(1)}, bf16[256,128]{1,0:T(8,128)(2,1)S(1)}, u32[]{:S(2)}, u32[]{:S(2)}) %collective-permute-start.21) | collective-permute-done | bytes 65568 | tf_op jit(solution)/shard_map/ppermute | solution.py:22
  61.7 2.4 %collective-permute-done.22 = bf16[256,128]{1,0:T(8,128)(2,1)S(1)} collective-permute-done((bf16[256,128]{1,0:T(8,128)(2,1)S(1)}, bf16[256,128]{1,0:T(8,128)(2,1)S(1)}, u32[]{:S(2)}, u32[]{:S(2)}) %collective-permute-start.22) | collective-permute-done | bytes 65568 | tf_op jit(solution)/shard_map/ppermute | solution.py:22
  64.1 0.9 %collective-permute-start.28 = (bf16[256,128]{1,0:T(8,128)(2,1)S(1)}, bf16[256,128]{1,0:T(8,128)(2,1)S(1)}, u32[]{:S(2)}, u32[]{:S(2)}) collective-permute-start(bf16[256,128]{1,0:T(8,128)(2,1)S(1)} %fusion.7.refs_0_), channel_id=1, source_target_pairs={{0,16},{8,24},{16,0},{24,8},{1,17},{9,25},{17,1},{25,9},{2,18},{10... | collective-permute-start | bytes 196616 | tf_op jit(solution)/shard_map/ppermute | solution.py:22
  65.0 0.6 collective-permute-start.29
  65.7 0.7 collective-permute-start.26
  66.4 1.7 %shard_map.86.lag_ref = f32[9,2,512,128]{3,2,1,0:T(8,128)S(1)} custom-call(bf16[1024,256]{1,0:T(8,128)(2,1)S(1)} %copy-done, bf16[2,512,128]{2,1,0:T(8,128)(2,1)S(1)} %pad_maximum_fusion.3.refs_0_, bf16[2,512,128]{2,1,0:T(8,128)(2,1)S(1)} %collective-permute-done.refs_1_, bf16[2,512,128]{2,1,0:T(8,128)(2,1)S(1)} %collective-permute-done.1.refs_2_, ...), custom_call_target="tpu_custom_call" | custom-call | flops 1073741824 | bytes 6291456 | tf_op jit(solution)/shard_map/pallas_call | solution.py:173
  68.1 0.9 %collective-permute-start.24 = (bf16[256,128]{1,0:T(8,128)(2,1)S(1)}, bf16[256,128]{1,0:T(8,128)(2,1)S(1)}, u32[]{:S(2)}, u32[]{:S(2)}) collective-permute-start(bf16[256,128]{1,0:T(8,128)(2,1)S(1)} %fusion.3.refs_0_), channel_id=1, source_target_pairs={{0,16},{8,24},{16,0},{24,8},{1,17},{9,25},{17,1},{25,9},{2,18},{10... | collective-permute-start | bytes 196616 | tf_op jit(solution)/shard_map/ppermute | solution.py:22
  69.6 1.2 %shard_map.91.refs_2_ = f32[512,512]{1,0:T(8,128)S(1)} custom-call(bf16[1024,256]{1,0:T(8,128)(2,1)S(1)} %copy-done, f32[9,2,512,128]{3,2,1,0:T(8,128)S(1)} %shard_map.86.lag_ref, bf16[256,128]{1,0:T(8,128)(2,1)S(1)} %fusion.7.refs_0_, bf16[256,128]{1,0:T(8,128)(2,1)S(1)} %collective-permute-done.27.refs_1_, ...), custom_call_target="tpu_custom_call" | custom-call | flops 536870912 | bytes 4194304 | tf_op jit(solution)/shard_map/pallas_call | solution.py:251
  71.4 1.5 %collective-permute-done.24.refs_0_ = bf16[256,128]{1,0:T(8,128)(2,1)S(1)} collective-permute-done((bf16[256,128]{1,0:T(8,128)(2,1)S(1)}, bf16[256,128]{1,0:T(8,128)(2,1)S(1)}, u32[]{:S(2)}, u32[]{:S(2)}) %collective-permute-start.24) | collective-permute-done | bytes 65568 | tf_op jit(solution)/shard_map/ppermute | solution.py:22
  73.4 1.7 %shard_map.93 = (bf16[512,128]{1,0:T(8,128)(2,1)}, f32[512,128]{1,0:T(8,128)}) custom-call(bf16[1024,256]{1,0:T(8,128)(2,1)S(1)} %copy-done, f32[9,2,512,128]{3,2,1,0:T(8,128)S(1)} %shard_map.86.lag_ref, bf16[256,128]{1,0:T(8,128)(2,1)S(1)} %collective-permute-done.24.refs_0_, bf16[256,128]{1,0:T(8,128)(2,1)S(1)} %collective-permute-done.25.refs_1_, ...), custom_call_target="tpu_custom_call" | custom-call | flops 268435456 | bytes 4194304 | tf_op jit(solution)/shard_map/pallas_call | solution.py:251
  (61 shorter events, 6.7 us)
Async XLA Ops:
  2.0 8.7 %collective-permute-start.8 = (bf16[128,256]{1,0:T(8,128)(2,1)S(1)}, bf16[128,256]{1,0:T(8,128)(2,1)S(1)}, u32[]{:S(2)}, u32[]{:S(2)}) collective-permute-start(bf16[128,256]{1,0:T(8,128)(2,1)S(1)} %get-tuple-element.27), channel_id=1, source_target_pairs={{0,5},{1,4},{2,7},{3,6},{4,1},{5,0},{6,3},{7,2},{8,13},{9,12},{10,... | collective-permute-start | bytes 196616 | tf_op jit(solution)/shard_map/ppermute | solution.py:22
  7.1 9.0 %collective-permute-start.6 = (bf16[128,256]{1,0:T(8,128)(2,1)S(1)}, bf16[128,256]{1,0:T(8,128)(2,1)S(1)}, u32[]{:S(2)}, u32[]{:S(2)}) collective-permute-start(bf16[128,256]{1,0:T(8,128)(2,1)S(1)} %get-tuple-element.26), channel_id=1, source_target_pairs={{0,7},{1,6},{2,5},{3,4},{4,3},{5,2},{6,1},{7,0},{8,15},{9,14},{10,... | collective-permute-start | bytes 196616 | tf_op jit(solution)/shard_map/ppermute | solution.py:22
  10.8 5.9 %collective-permute-start.9 = (bf16[128,256]{1,0:T(8,128)(2,1)S(1)}, bf16[128,256]{1,0:T(8,128)(2,1)S(1)}, u32[]{:S(2)}, u32[]{:S(2)}) collective-permute-start(bf16[128,256]{1,0:T(8,128)(2,1)S(1)} %collective-permute-done.8), channel_id=1, source_target_pairs={{0,16},{8,24},{16,0},{24,8},{1,17},{9,25},{17,1},{25,9},{2,18},{10... | collective-permute-start | bytes 196616 | tf_op jit(solution)/shard_map/ppermute | solution.py:22
  12.4 6.0 %collective-permute-start.12 = (bf16[128,512]{1,0:T(8,128)(2,1)S(1)}, bf16[128,512]{1,0:T(8,128)(2,1)S(1)}, u32[]{:S(2)}, u32[]{:S(2)}) collective-permute-start(bf16[128,512]{1,0:T(8,128)(2,1)S(1)} %get-tuple-element.28), channel_id=1, source_target_pairs={{0,3},{1,2},{2,1},{3,0},{4,7},{5,6},{6,5},{7,4},{8,11},{9,10},{10,... | collective-permute-start | bytes 393224 | tf_op jit(solution)/shard_map/ppermute | solution.py:22
  14.5 5.3 %collective-permute-start.13 = (bf16[128,512]{1,0:T(8,128)(2,1)S(1)}, bf16[128,512]{1,0:T(8,128)(2,1)S(1)}, u32[]{:S(2)}, u32[]{:S(2)}) collective-permute-start(bf16[128,512]{1,0:T(8,128)(2,1)S(1)} %get-tuple-element.29), channel_id=1, source_target_pairs={{0,1},{1,0},{2,3},{3,2},{4,5},{5,4},{6,7},{7,6},{8,9},{9,8},{10,11... | collective-permute-start | bytes 393224 | tf_op jit(solution)/shard_map/ppermute | solution.py:22
  16.1 4.3 %collective-permute-start.7 = (bf16[128,256]{1,0:T(8,128)(2,1)S(1)}, bf16[128,256]{1,0:T(8,128)(2,1)S(1)}, u32[]{:S(2)}, u32[]{:S(2)}) collective-permute-start(bf16[128,256]{1,0:T(8,128)(2,1)S(1)} %collective-permute-done.6), channel_id=1, source_target_pairs={{0,16},{8,24},{16,0},{24,8},{1,17},{9,25},{17,1},{25,9},{2,18},{10... | collective-permute-start | bytes 196616 | tf_op jit(solution)/shard_map/ppermute | solution.py:22
  16.6 9.8 %collective-permute-start.11 = (bf16[2,128,256]{2,1,0:T(8,128)(2,1)S(1)}, bf16[2,128,256]{2,1,0:T(8,128)(2,1)S(1)}, u32[]{:S(2)}, u32[]{:S(2)}) collective-permute-start(bf16[2,128,256]{2,1,0:T(8,128)(2,1)S(1)} %get-tuple-element.51), channel_id=1, source_target_pairs={{0,8},{8,0},{16,24},{24,16},{1,9},{9,1},{17,25},{25,17},{2,10},{10... | collective-permute-start | bytes 393224 | tf_op jit(solution)/shard_map/ppermute | solution.py:22
  19.8 7.4 %collective-permute-start.14 = (bf16[2,128,512]{2,1,0:T(8,128)(2,1)S(1)}, bf16[2,128,512]{2,1,0:T(8,128)(2,1)S(1)}, u32[]{:S(2)}, u32[]{:S(2)}) collective-permute-start(bf16[2,128,512]{2,1,0:T(8,128)(2,1)S(1)} %pad_maximum_fusion.6.refs_4_), channel_id=1, source_target_pairs={{0,8},{8,0},{16,24},{24,16},{1,9},{9,1},{17,25},{25,17},{2,10},{10... | collective-permute-start | bytes 786440 | tf_op jit(solution)/shard_map/ppermute | solution.py:22
  20.4 6.7 %collective-permute-start.10 = (bf16[2,128,256]{2,1,0:T(8,128)(2,1)S(1)}, bf16[2,128,256]{2,1,0:T(8,128)(2,1)S(1)}, u32[]{:S(2)}, u32[]{:S(2)}) collective-permute-start(bf16[2,128,256]{2,1,0:T(8,128)(2,1)S(1)} %get-tuple-element.49), channel_id=1, source_target_pairs={{0,8},{8,0},{16,24},{24,16},{1,9},{9,1},{17,25},{25,17},{2,10},{10... | collective-permute-start | bytes 393224 | tf_op jit(solution)/shard_map/ppermute | solution.py:22
  20.5 8.9 %collective-permute-start.3 = (bf16[128,512]{1,0:T(8,128)(2,1)S(1)}, bf16[128,512]{1,0:T(8,128)(2,1)S(1)}, u32[]{:S(2)}, u32[]{:S(2)}) collective-permute-start(bf16[128,512]{1,0:T(8,128)(2,1)S(1)} %get-tuple-element.23), channel_id=1, source_target_pairs={{0,6},{1,7},{2,4},{3,5},{4,2},{5,3},{6,0},{7,1},{8,14},{9,15},{10,... | collective-permute-start | bytes 393224 | tf_op jit(solution)/shard_map/ppermute | solution.py:22
  25.1 12.2 %collective-permute-start.4 = (bf16[128,512]{1,0:T(8,128)(2,1)S(1)}, bf16[128,512]{1,0:T(8,128)(2,1)S(1)}, u32[]{:S(2)}, u32[]{:S(2)}) collective-permute-start(bf16[128,512]{1,0:T(8,128)(2,1)S(1)} %get-tuple-element.24), channel_id=1, source_target_pairs={{0,4},{1,5},{2,6},{3,7},{4,0},{5,1},{6,2},{7,3},{8,12},{9,13},{10,... | collective-permute-start | bytes 393224 | tf_op jit(solution)/shard_map/ppermute | solution.py:22
  26.5 10.8 %collective-permute-start.5 = (bf16[128,512]{1,0:T(8,128)(2,1)S(1)}, bf16[128,512]{1,0:T(8,128)(2,1)S(1)}, u32[]{:S(2)}, u32[]{:S(2)}) collective-permute-start(bf16[128,512]{1,0:T(8,128)(2,1)S(1)} %get-tuple-element.25), channel_id=1, source_target_pairs={{0,2},{1,3},{2,0},{3,1},{4,6},{5,7},{6,4},{7,5},{8,10},{9,11},{10,... | collective-permute-start | bytes 393224 | tf_op jit(solution)/shard_map/ppermute | solution.py:22
  27.2 30.5 %copy-start.4 = (bf16[512,128]{1,0:T(8,128)(2,1)S(1)}, bf16[512,128]{1,0:T(8,128)(2,1)}, u32[]{:S(2)}) copy-start(bf16[512,128]{1,0:T(8,128)(2,1)} %param.9) | copy-start | bytes 393220
  28.0 38.5 %copy-start = (bf16[1024,256]{1,0:T(8,128)(2,1)S(1)}, bf16[1024,256]{1,0:T(8,128)(2,1)}, u32[]{:S(2)}) copy-start(bf16[1024,256]{1,0:T(8,128)(2,1)} %constant.4.clone.dft_ref) | copy-start | bytes 1572868
  37.3 2.2 %collective-permute-start.15 = (bf16[3,128,512]{2,1,0:T(8,128)(2,1)S(1)}, bf16[3,128,512]{2,1,0:T(8,128)(2,1)S(1)}, u32[]{:S(2)}, u32[]{:S(2)}) collective-permute-start(bf16[3,128,512]{2,1,0:T(8,128)(2,1)S(1)} %pad_maximum_fusion.2), channel_id=1, source_target_pairs={{0,8},{8,0},{16,24},{24,16},{1,9},{9,1},{17,25},{25,17},{2,10},{10... | collective-permute-start | bytes 1179656 | tf_op jit(solution)/shard_map/ppermute | solution.py:22
  37.5 9.2 %collective-permute-start.16 = (bf16[4,256,128]{2,1,0:T(8,128)(2,1)S(1)}, bf16[4,256,128]{2,1,0:T(8,128)(2,1)S(1)}, u32[]{:S(2)}, u32[]{:S(2)}) collective-permute-start(bf16[4,256,128]{2,1,0:T(8,128)(2,1)S(1)} %get-tuple-element.30), channel_id=1, source_target_pairs={{0,1},{1,0},{2,3},{3,2},{4,5},{5,4},{6,7},{7,6},{8,9},{9,8},{10,11... | collective-permute-start | bytes 786440 | tf_op jit(solution)/shard_map/ppermute | solution.py:22
  38.1 13.7 %collective-permute-start.20 = (bf16[4,256,128]{2,1,0:T(8,128)(2,1)S(1)}, bf16[4,256,128]{2,1,0:T(8,128)(2,1)S(1)}, u32[]{:S(2)}, u32[]{:S(2)}) collective-permute-start(bf16[4,256,128]{2,1,0:T(8,128)(2,1)S(1)} %get-tuple-element.39), channel_id=1, source_target_pairs={{0,1},{1,0},{2,3},{3,2},{4,5},{5,4},{6,7},{7,6},{8,9},{9,8},{10,11... | collective-permute-start | bytes 786440 | tf_op jit(solution)/shard_map/ppermute | solution.py:22
  46.7 6.1 %collective-permute-start.17 = (bf16[256,128]{1,0:T(8,128)(2,1)S(1)}, bf16[256,128]{1,0:T(8,128)(2,1)S(1)}, u32[]{:S(2)}, u32[]{:S(2)}) collective-permute-start(bf16[256,128]{1,0:T(8,128)(2,1)S(1)} %get-tuple-element.46), channel_id=1, source_target_pairs={{0,6},{1,7},{2,4},{3,5},{4,2},{5,3},{6,0},{7,1},{8,14},{9,15},{10,... | collective-permute-start | bytes 196616 | tf_op jit(solution)/shard_map/ppermute | solution.py:22
  49.5 5.4 %collective-permute-start.18 = (bf16[256,128]{1,0:T(8,128)(2,1)S(1)}, bf16[256,128]{1,0:T(8,128)(2,1)S(1)}, u32[]{:S(2)}, u32[]{:S(2)}) collective-permute-start(bf16[256,128]{1,0:T(8,128)(2,1)S(1)} %get-tuple-element.48), channel_id=1, source_target_pairs={{0,4},{1,5},{2,6},{3,7},{4,0},{5,1},{6,2},{7,3},{8,12},{9,13},{10,... | collective-permute-start | bytes 196616 | tf_op jit(solution)/shard_map/ppermute | solution.py:22
  49.5 5.4 %collective-permute-start.19 = (bf16[256,128]{1,0:T(8,128)(2,1)S(1)}, bf16[256,128]{1,0:T(8,128)(2,1)S(1)}, u32[]{:S(2)}, u32[]{:S(2)}) collective-permute-start(bf16[256,128]{1,0:T(8,128)(2,1)S(1)} %get-tuple-element.47), channel_id=1, source_target_pairs={{0,2},{1,3},{2,0},{3,1},{4,6},{5,7},{6,4},{7,5},{8,10},{9,11},{10,... | collective-permute-start | bytes 196616 | tf_op jit(solution)/shard_map/ppermute | solution.py:22
  51.8 5.3 %collective-permute-start.23 = (bf16[256,128]{1,0:T(8,128)(2,1)S(1)}, bf16[256,128]{1,0:T(8,128)(2,1)S(1)}, u32[]{:S(2)}, u32[]{:S(2)}) collective-permute-start(bf16[256,128]{1,0:T(8,128)(2,1)S(1)} %fusion.13), channel_id=1, source_target_pairs={{0,2},{1,3},{2,0},{3,1},{4,6},{5,7},{6,4},{7,5},{8,10},{9,11},{10,... | collective-permute-start | bytes 196616 | tf_op jit(solution)/shard_map/ppermute | solution.py:22
  51.9 13.1 %collective-permute-start = (bf16[2,512,128]{2,1,0:T(8,128)(2,1)S(1)}, bf16[2,512,128]{2,1,0:T(8,128)(2,1)S(1)}, u32[]{:S(2)}, u32[]{:S(2)}) collective-permute-start(bf16[2,512,128]{2,1,0:T(8,128)(2,1)S(1)} %pad_maximum_fusion.3.refs_0_), channel_id=1, source_target_pairs={{0,8},{8,0},{16,24},{24,16},{1,9},{9,1},{17,25},{25,17},{2,10},{10... | collective-permute-start | bytes 786440 | tf_op jit(solution)/shard_map/ppermute | solution.py:22
  52.8 12.8 %collective-permute-start.1 = (bf16[2,512,128]{2,1,0:T(8,128)(2,1)S(1)}, bf16[2,512,128]{2,1,0:T(8,128)(2,1)S(1)}, u32[]{:S(2)}, u32[]{:S(2)}) collective-permute-start(bf16[2,512,128]{2,1,0:T(8,128)(2,1)S(1)} %pad_maximum_fusion.3.refs_0_), channel_id=1, source_target_pairs={{0,16},{8,24},{16,0},{24,8},{1,17},{9,25},{17,1},{25,9},{2,18},{10... | collective-permute-start | bytes 786440 | tf_op jit(solution)/shard_map/ppermute | solution.py:22
  54.9 11.5 %collective-permute-start.2 = (bf16[2,512,128]{2,1,0:T(8,128)(2,1)S(1)}, bf16[2,512,128]{2,1,0:T(8,128)(2,1)S(1)}, u32[]{:S(2)}, u32[]{:S(2)}) collective-permute-start(bf16[2,512,128]{2,1,0:T(8,128)(2,1)S(1)} %pad_maximum_fusion.3.refs_0_), channel_id=1, source_target_pairs={{0,24},{8,16},{16,8},{24,0},{1,25},{9,17},{17,9},{25,1},{2,26},{10... | collective-permute-start | bytes 786440 | tf_op jit(solution)/shard_map/ppermute | solution.py:22
  54.9 6.8 %collective-permute-start.21 = (bf16[256,128]{1,0:T(8,128)(2,1)S(1)}, bf16[256,128]{1,0:T(8,128)(2,1)S(1)}, u32[]{:S(2)}, u32[]{:S(2)}) collective-permute-start(bf16[256,128]{1,0:T(8,128)(2,1)S(1)} %get-tuple-element.45), channel_id=1, source_target_pairs={{0,6},{1,7},{2,4},{3,5},{4,2},{5,3},{6,0},{7,1},{8,14},{9,15},{10,... | collective-permute-start | bytes 196616 | tf_op jit(solution)/shard_map/ppermute | solution.py:22
  57.1 7.0 %collective-permute-start.22 = (bf16[256,128]{1,0:T(8,128)(2,1)S(1)}, bf16[256,128]{1,0:T(8,128)(2,1)S(1)}, u32[]{:S(2)}, u32[]{:S(2)}) collective-permute-start(bf16[256,128]{1,0:T(8,128)(2,1)S(1)} %get-tuple-element.44), channel_id=1, source_target_pairs={{0,4},{1,5},{2,6},{3,7},{4,0},{5,1},{6,2},{7,3},{8,12},{9,13},{10,... | collective-permute-start | bytes 196616 | tf_op jit(solution)/shard_map/ppermute | solution.py:22
  61.7 7.3 %collective-permute-start.27 = (bf16[256,128]{1,0:T(8,128)(2,1)S(1)}, bf16[256,128]{1,0:T(8,128)(2,1)S(1)}, u32[]{:S(2)}, u32[]{:S(2)}) collective-permute-start(bf16[256,128]{1,0:T(8,128)(2,1)S(1)} %fusion.7.refs_0_), channel_id=1, source_target_pairs={{0,8},{8,0},{16,24},{24,16},{1,9},{9,1},{17,25},{25,17},{2,10},{10... | collective-permute-start | bytes 196616 | tf_op jit(solution)/shard_map/ppermute | solution.py:22
  64.1 5.4 %collective-permute-start.28 = (bf16[256,128]{1,0:T(8,128)(2,1)S(1)}, bf16[256,128]{1,0:T(8,128)(2,1)S(1)}, u32[]{:S(2)}, u32[]{:S(2)}) collective-permute-start(bf16[256,128]{1,0:T(8,128)(2,1)S(1)} %fusion.7.refs_0_), channel_id=1, source_target_pairs={{0,16},{8,24},{16,0},{24,8},{1,17},{9,25},{17,1},{25,9},{2,18},{10... | collective-permute-start | bytes 196616 | tf_op jit(solution)/shard_map/ppermute | solution.py:22
  65.0 4.5 %collective-permute-start.29 = (bf16[256,128]{1,0:T(8,128)(2,1)S(1)}, bf16[256,128]{1,0:T(8,128)(2,1)S(1)}, u32[]{:S(2)}, u32[]{:S(2)}) collective-permute-start(bf16[256,128]{1,0:T(8,128)(2,1)S(1)} %fusion.7.refs_0_), channel_id=1, source_target_pairs={{0,24},{8,16},{16,8},{24,0},{1,25},{9,17},{17,9},{25,1},{2,26},{10... | collective-permute-start | bytes 196616 | tf_op jit(solution)/shard_map/ppermute | solution.py:22
  65.7 5.1 %collective-permute-start.26 = (bf16[256,128]{1,0:T(8,128)(2,1)S(1)}, bf16[256,128]{1,0:T(8,128)(2,1)S(1)}, u32[]{:S(2)}, u32[]{:S(2)}) collective-permute-start(bf16[256,128]{1,0:T(8,128)(2,1)S(1)} %fusion.3.refs_0_), channel_id=1, source_target_pairs={{0,8},{8,0},{16,24},{24,16},{1,9},{9,1},{17,25},{25,17},{2,10},{10... | collective-permute-start | bytes 196616 | tf_op jit(solution)/shard_map/ppermute | solution.py:22
  68.1 4.8 %collective-permute-start.24 = (bf16[256,128]{1,0:T(8,128)(2,1)S(1)}, bf16[256,128]{1,0:T(8,128)(2,1)S(1)}, u32[]{:S(2)}, u32[]{:S(2)}) collective-permute-start(bf16[256,128]{1,0:T(8,128)(2,1)S(1)} %fusion.3.refs_0_), channel_id=1, source_target_pairs={{0,16},{8,24},{16,0},{24,8},{1,17},{9,25},{17,1},{25,9},{2,18},{10... | collective-permute-start | bytes 196616 | tf_op jit(solution)/shard_map/ppermute | solution.py:22
  69.0 4.4 %collective-permute-start.25 = (bf16[256,128]{1,0:T(8,128)(2,1)S(1)}, bf16[256,128]{1,0:T(8,128)(2,1)S(1)}, u32[]{:S(2)}, u32[]{:S(2)}) collective-permute-start(bf16[256,128]{1,0:T(8,128)(2,1)S(1)} %fusion.3.refs_0_), channel_id=1, source_target_pairs={{0,24},{8,16},{16,8},{24,0},{1,25},{9,17},{17,9},{25,1},{2,26},{10... | collective-permute-start | bytes 196616 | tf_op jit(solution)/shard_map/ppermute | solution.py:22
  (3 other events, 52.1 us)

commit v2 on v1

--- a/solution.py
+++ b/solution.py
@@ -106,7 +106,7 @@
 
 def product_kernel(sizes, d_ref, *refs):
     parts, outs = refs[: len(sizes)], refs[len(sizes) :]
-    count = outs[0].shape[0]
+    count = 2 * outs[0].shape[0]
     channels = outs[0].shape[-1]
     for which in range(2):
         rows = pl.ds(which * SUB, SUB)
@@ -123,8 +123,9 @@
                 w = jnp.concatenate([part[(*index, i - first)], part[(*index, i + 1 - first)]], axis=0)
                 term = lax.dot_general(left, w, NT, preferred_element_type=F32)
                 total = term if total is None else total + term
-            outs[which][i] = total[:, :channels].astype(outs[which].dtype)
-            outs[which][i + 1] = total[:, channels:].astype(outs[which].dtype)
+            out_ref, at = outs[2 * which + 2 * i // count], i % (count // 2)
+            out_ref[at] = total[:, :channels].astype(out_ref.dtype)
+            out_ref[at + 1] = total[:, channels:].astype(out_ref.dtype)
 
 
 def product(d_out, parts, out_type):
@@ -133,9 +134,9 @@
     sizes = [(index, first, block.shape[-3], whose) for block, index, first, whose in parts]
     return pl.pallas_call(
         functools.partial(product_kernel, sizes),
-        out_shape=(jax.ShapeDtypeStruct((count, SUB, channels), out_type),) * 2,
+        out_shape=(jax.ShapeDtypeStruct((count // 2, SUB, channels), out_type),) * 4,
         in_specs=[VMEM] * (1 + len(parts)),
-        out_specs=(VMEM, VMEM),
+        out_specs=(VMEM,) * 4,
         compiler_params=pltpu.CompilerParams(vmem_limit_bytes=8 << 20),
         cost_estimate=pl.CostEstimate(
             flops=4 * count * SUB * channels * d_out.shape[1], bytes_accessed=4 << 20, transcendentals=0
@@ -261,8 +262,8 @@
     )(*args)
 
 
-def spread_offsets(size):
-    if size <= 4:
+def spread_offsets(size, direct=True):
+    if direct and size <= 4:
         return [(offset, 0, offset) for offset in reversed(range(1, size))]
     held, moves, mask = [0], [], size // 2
     while mask:
@@ -273,10 +274,10 @@
     return moves
 
 
-def spread_blocks(block, axis):
+def spread_blocks(block, axis, direct=True):
     size = lax.axis_size(axis)
     held = {0: block}
-    for offset, source, mask in spread_offsets(size):
+    for offset, source, mask in spread_offsets(size, direct):
         held[offset] = swapped(held[source], axis, mask)
     return held
 
@@ -314,7 +315,7 @@
     twin = swapped(near, "seq", 1)
     odd_parts += [(near, (), far, (False, 0, 0)), (twin, (), far, (False, 1, 0))]
     lag_pair = jnp.stack([filt, inner])
-    lag_blocks = [block for _, block in sorted(spread_blocks(lag_pair, "seq").items())]
+    lag_blocks = [block for _, block in sorted(spread_blocks(lag_pair, "seq", False).items())]
     dft, back = dft_parts()
 
     p_odd = product(d_out, odd_parts, BF16)
@@ -325,19 +326,18 @@
         (jnp.concatenate([near, blocks[-2][None]]), (), 0, (False, 0, 0)),
         (jnp.concatenate([twin, blocks[-1][None]]), (), 0, (False, 1, 0)),
     ]
-    from_pair = [swapped(p_odd[which], "chan", 1) for which in range(2)]
+    from_pair = [swapped(block, "chan", 1) for block in p_odd]
     lags = lag_spectra(dft, lag_blocks)
     p_even = product(d_out, even_parts, F32)
-    own, parts = [], []
+    own, parts, size = [], [], groups // 2
     for which in range(2):
-        mine, theirs = p_even[which], from_pair[which]
         sent = []
-        for i, mask in enumerate(even):
-            if which and i == groups - 2:
-                mine, theirs, *_ = lax.optimization_barrier((mine, theirs, *sent))
-            total = mine[i] + theirs[i].astype(F32)
-            sent.append(total.astype(BF16) if mask else total)
-        own.append(sent.pop())
+        for kind in range(2):
+            mine, theirs = p_even[2 * which + kind], from_pair[2 * which + kind]
+            totals = [mine[i] + theirs[i].astype(F32) for i in range(size)]
+            if kind:
+                own.append(totals.pop())
+            sent += [total.astype(BF16) for total in totals]
         parts.append([swapped(block, "chan", mask) for block, mask in zip(sent, even)])
     grad_blocks = []
     for which in range(2):

time: 75.3 us -> 83.6 us (1.11)
  waiting for transfers between devices: 32.8 us -> 37.1 us
  starting transfers between devices: 31.5 us -> 35.5 us
    ppermute x30 -> x32, waiting for transfers between devices: 32.8 us -> 37.1 us  [swapped(): return lax.ppermute(block, axis, [(i, i ^ mask) for i in range(size)])]
    ppermute x30 -> x32, starting transfers between devices: 31.5 us -> 35.5 us  [swapped(): return lax.ppermute(block, axis, [(i, i ^ mask) for i in range(size)])]
  transfers between devices with their start and end apart: 30 -> 32, of which waited for: 14 -> 13; matrix products, arithmetic and copies ran while one was open for 1% -> 1% of each run, Pallas kernels for 8% -> 7%
where the time goes in v2:
time: 83.6 us; the launch traced here: 83.4 us
  waiting for transfers between devices  37.1 us (44%)
  starting transfers between devices  35.5 us (42%)
  Pallas kernels  9.38 us (11%)
  between operations  0.91 us (1%)
    ppermute x32, waiting for transfers between devices, swapped(): return lax.ppermute(block, axis, [(i, i ^ mask) for i in range(size)])  37.1 us
    ppermute x32, starting transfers between devices, swapped(): return lax.ppermute(block, axis, [(i, i ^ mask) for i in range(size)])  35.5 us
    pallas_call x3, Pallas kernels, add_blocks(): pl.pallas_call(functools.partial(add_kernel, offsets, which, first, last)...  3.56 us
    pallas_call x1, Pallas kernels, lag_spectra(): pl.pallas_call(functools.partial(lag_kernel, n), out_shape=jax.ShapeDtype...  1.69 us
  transfers between devices with their start and end apart: 32, of which 13 were waited for; matrix products, arithmetic and copies ran while one was open for 1% of the time, Pallas kernels for 7%

profile of v2, /device:TPU:0, one launch (start us, length us, event | category | flops | bytes accessed | tf_op | source)
XLA Modules:
  0.0 83.4 jit_solution(12696426570863355902)
XLA Ops:
  0.6 1.4 %shard_map.88 = (bf16[128,256]{1,0:T(8,128)(2,1)S(1)}, bf16[128,256]{1,0:T(8,128)(2,1)S(1)}, bf16[128,512]{1,0:T(8,128)(2,1)S(1)}, bf16[128,512]{1,0:T(8,128)(2,...) custom-call(bf16[128,8192]{1,0:T(8,128)(2,1)} %w_ref.1), custom_call_target="tpu_custom_call" | custom-call | bytes 4194304 | tf_op jit(solution)/shard_map/pallas_call | solution.py:63
  2.1 5.1 %collective-permute-start.8 = (bf16[128,256]{1,0:T(8,128)(2,1)S(1)}, bf16[128,256]{1,0:T(8,128)(2,1)S(1)}, u32[]{:S(2)}, u32[]{:S(2)}) collective-permute-start(bf16[128,256]{1,0:T(8,128)(2,1)S(1)} %get-tuple-element.29), channel_id=1, source_target_pairs={{0,5},{1,4},{2,7},{3,6},{4,1},{5,0},{6,3},{7,2},{8,13},{9,12},{10,... | collective-permute-start | bytes 196616 | tf_op jit(solution)/shard_map/ppermute | solution.py:22
  7.1 1.3 %collective-permute-start.6 = (bf16[128,256]{1,0:T(8,128)(2,1)S(1)}, bf16[128,256]{1,0:T(8,128)(2,1)S(1)}, u32[]{:S(2)}, u32[]{:S(2)}) collective-permute-start(bf16[128,256]{1,0:T(8,128)(2,1)S(1)} %get-tuple-element.28), channel_id=1, source_target_pairs={{0,7},{1,6},{2,5},{3,4},{4,3},{5,2},{6,1},{7,0},{8,15},{9,14},{10,... | collective-permute-start | bytes 196616 | tf_op jit(solution)/shard_map/ppermute | solution.py:22
  8.4 2.4 %collective-permute-done.8 = bf16[128,256]{1,0:T(8,128)(2,1)S(1)} collective-permute-done((bf16[128,256]{1,0:T(8,128)(2,1)S(1)}, bf16[128,256]{1,0:T(8,128)(2,1)S(1)}, u32[]{:S(2)}, u32[]{:S(2)}) %collective-permute-start.8) | collective-permute-done | bytes 65568 | tf_op jit(solution)/shard_map/ppermute | solution.py:22
  10.8 1.6 %collective-permute-start.9 = (bf16[128,256]{1,0:T(8,128)(2,1)S(1)}, bf16[128,256]{1,0:T(8,128)(2,1)S(1)}, u32[]{:S(2)}, u32[]{:S(2)}) collective-permute-start(bf16[128,256]{1,0:T(8,128)(2,1)S(1)} %collective-permute-done.8), channel_id=1, source_target_pairs={{0,16},{8,24},{16,0},{24,8},{1,17},{9,25},{17,1},{25,9},{2,18},{10... | collective-permute-start | bytes 196616 | tf_op jit(solution)/shard_map/ppermute | solution.py:22
  12.4 2.0 %collective-permute-start.12 = (bf16[128,512]{1,0:T(8,128)(2,1)S(1)}, bf16[128,512]{1,0:T(8,128)(2,1)S(1)}, u32[]{:S(2)}, u32[]{:S(2)}) collective-permute-start(bf16[128,512]{1,0:T(8,128)(2,1)S(1)} %get-tuple-element.30), channel_id=1, source_target_pairs={{0,3},{1,2},{2,1},{3,0},{4,7},{5,6},{6,5},{7,4},{8,11},{9,10},{10,... | collective-permute-start | bytes 393224 | tf_op jit(solution)/shard_map/ppermute | solution.py:22
  14.5 1.6 %collective-permute-start.13 = (bf16[128,512]{1,0:T(8,128)(2,1)S(1)}, bf16[128,512]{1,0:T(8,128)(2,1)S(1)}, u32[]{:S(2)}, u32[]{:S(2)}) collective-permute-start(bf16[128,512]{1,0:T(8,128)(2,1)S(1)} %get-tuple-element.31), channel_id=1, source_target_pairs={{0,1},{1,0},{2,3},{3,2},{4,5},{5,4},{6,7},{7,6},{8,9},{9,8},{10,11... | collective-permute-start | bytes 393224 | tf_op jit(solution)/shard_map/ppermute | solution.py:22
  16.7 1.7 %collective-permute-done.12 = bf16[128,512]{1,0:T(8,128)(2,1)S(1)} collective-permute-done((bf16[128,512]{1,0:T(8,128)(2,1)S(1)}, bf16[128,512]{1,0:T(8,128)(2,1)S(1)}, u32[]{:S(2)}, u32[]{:S(2)}) %collective-permute-start.12) | collective-permute-done | bytes 131104 | tf_op jit(solution)/shard_map/ppermute | solution.py:22
  18.4 1.4 %collective-permute-done.13 = bf16[128,512]{1,0:T(8,128)(2,1)S(1)} collective-permute-done((bf16[128,512]{1,0:T(8,128)(2,1)S(1)}, bf16[128,512]{1,0:T(8,128)(2,1)S(1)}, u32[]{:S(2)}, u32[]{:S(2)}) %collective-permute-start.13) | collective-permute-done | bytes 131104 | tf_op jit(solution)/shard_map/ppermute | solution.py:22
  20.5 4.6 %collective-permute-start.3 = (bf16[128,512]{1,0:T(8,128)(2,1)S(1)}, bf16[128,512]{1,0:T(8,128)(2,1)S(1)}, u32[]{:S(2)}, u32[]{:S(2)}) collective-permute-start(bf16[128,512]{1,0:T(8,128)(2,1)S(1)} %get-tuple-element.25), channel_id=1, source_target_pairs={{0,6},{1,7},{2,4},{3,5},{4,2},{5,3},{6,0},{7,1},{8,14},{9,15},{10,... | collective-permute-start | bytes 393224 | tf_op jit(solution)/shard_map/ppermute | solution.py:22
  25.2 1.2 %shard_map.87.d_ref = bf16[512,1024]{1,0:T(8,128)(2,1)S(1)} custom-call(bf16[512,1024]{1,0:T(8,128)(2,1)} %source_ref.1), custom_call_target="tpu_custom_call" | custom-call | bytes 2097152 | tf_op jit(solution)/shard_map/pallas_call | solution.py:90
  27.2 0.8 shard_map.89
  28.0 1.5 %collective-permute-done.3 = bf16[128,512]{1,0:T(8,128)(2,1)S(1)} collective-permute-done((bf16[128,512]{1,0:T(8,128)(2,1)S(1)}, bf16[128,512]{1,0:T(8,128)(2,1)S(1)}, u32[]{:S(2)}, u32[]{:S(2)}) %collective-permute-start.3) | collective-permute-done | bytes 131104 | tf_op jit(solution)/shard_map/ppermute | solution.py:22
  29.4 7.9 %collective-permute-done.4 = bf16[128,512]{1,0:T(8,128)(2,1)S(1)} collective-permute-done((bf16[128,512]{1,0:T(8,128)(2,1)S(1)}, bf16[128,512]{1,0:T(8,128)(2,1)S(1)}, u32[]{:S(2)}, u32[]{:S(2)}) %collective-permute-start.4) | collective-permute-done | bytes 131104 | tf_op jit(solution)/shard_map/ppermute | solution.py:22
  38.3 8.0 %collective-permute-done.1.refs_2_ = bf16[2,512,128]{2,1,0:T(8,128)(2,1)S(1)} collective-permute-done((bf16[2,512,128]{2,1,0:T(8,128)(2,1)S(1)}, bf16[2,512,128]{2,1,0:T(8,128)(2,1)S(1)}, u32[]{:S(2)}, u32[]{:S(2)}) %collective-permute-start.1) | collective-permute-done | bytes 262176 | tf_op jit(solution)/shard_map/ppermute | solution.py:22
  46.8 1.4 %collective-permute-start.16 = (bf16[2,256,128]{2,1,0:T(8,128)(2,1)S(1)}, bf16[2,256,128]{2,1,0:T(8,128)(2,1)S(1)}, u32[]{:S(2)}, u32[]{:S(2)}) collective-permute-start(bf16[2,256,128]{2,1,0:T(8,128)(2,1)S(1)} %get-tuple-element.39), channel_id=1, source_target_pairs={{0,1},{1,0},{2,3},{3,2},{4,5},{5,4},{6,7},{7,6},{8,9},{9,8},{10,11... | collective-permute-start | bytes 393224 | tf_op jit(solution)/shard_map/ppermute | solution.py:22
  49.1 0.8 shard_map.90
  49.8 2.8 %collective-permute-done.17 = bf16[2,256,128]{2,1,0:T(8,128)(2,1)S(1)} collective-permute-done((bf16[2,256,128]{2,1,0:T(8,128)(2,1)S(1)}, bf16[2,256,128]{2,1,0:T(8,128)(2,1)S(1)}, u32[]{:S(2)}, u32[]{:S(2)}) %collective-permute-start.17) | collective-permute-done | bytes 131104 | tf_op jit(solution)/shard_map/ppermute | solution.py:22
  53.2 5.0 %collective-permute-done.22 = bf16[2,256,128]{2,1,0:T(8,128)(2,1)S(1)} collective-permute-done((bf16[2,256,128]{2,1,0:T(8,128)(2,1)S(1)}, bf16[2,256,128]{2,1,0:T(8,128)(2,1)S(1)}, u32[]{:S(2)}, u32[]{:S(2)}) %collective-permute-start.22) | collective-permute-done | bytes 131104 | tf_op jit(solution)/shard_map/ppermute | solution.py:22
  58.2 2.7 %collective-permute-start.18 = (bf16[256,128]{1,0:T(8,128)(2,1)S(1)}, bf16[256,128]{1,0:T(8,128)(2,1)S(1)}, u32[]{:S(2)}, u32[]{:S(2)}) collective-permute-start(bf16[256,128]{1,0:T(8,128)(2,1)S(1)} %get-tuple-element.50), channel_id=1, source_target_pairs={{0,6},{1,7},{2,4},{3,5},{4,2},{5,3},{6,0},{7,1},{8,14},{9,15},{10,... | collective-permute-start | bytes 196616 | tf_op jit(solution)/shard_map/ppermute | solution.py:22
  61.1 1.7 %collective-permute-start.20 = (bf16[256,128]{1,0:T(8,128)(2,1)S(1)}, bf16[256,128]{1,0:T(8,128)(2,1)S(1)}, u32[]{:S(2)}, u32[]{:S(2)}) collective-permute-start(bf16[256,128]{1,0:T(8,128)(2,1)S(1)} %fusion.10), channel_id=1, source_target_pairs={{0,2},{1,3},{2,0},{3,1},{4,6},{5,7},{6,4},{7,5},{8,10},{9,11},{10,... | collective-permute-start | bytes 196616 | tf_op jit(solution)/shard_map/ppermute | solution.py:22
  62.9 1.6 %collective-permute-done.18 = bf16[256,128]{1,0:T(8,128)(2,1)S(1)} collective-permute-done((bf16[256,128]{1,0:T(8,128)(2,1)S(1)}, bf16[256,128]{1,0:T(8,128)(2,1)S(1)}, u32[]{:S(2)}, u32[]{:S(2)}) %collective-permute-start.18) | collective-permute-done | bytes 65568 | tf_op jit(solution)/shard_map/ppermute | solution.py:22
  64.5 2.9 %collective-permute-start.23 = (bf16[256,128]{1,0:T(8,128)(2,1)S(1)}, bf16[256,128]{1,0:T(8,128)(2,1)S(1)}, u32[]{:S(2)}, u32[]{:S(2)}) collective-permute-start(bf16[256,128]{1,0:T(8,128)(2,1)S(1)} %get-tuple-element.48), channel_id=1, source_target_pairs={{0,6},{1,7},{2,4},{3,5},{4,2},{5,3},{6,0},{7,1},{8,14},{9,15},{10,... | collective-permute-start | bytes 196616 | tf_op jit(solution)/shard_map/ppermute | solution.py:22
  67.4 2.4 %collective-permute-start.25 = (bf16[256,128]{1,0:T(8,128)(2,1)S(1)}, bf16[256,128]{1,0:T(8,128)(2,1)S(1)}, u32[]{:S(2)}, u32[]{:S(2)}) collective-permute-start(bf16[256,128]{1,0:T(8,128)(2,1)S(1)} %fusion.13), channel_id=1, source_target_pairs={{0,2},{1,3},{2,0},{3,1},{4,6},{5,7},{6,4},{7,5},{8,10},{9,11},{10,... | collective-permute-start | bytes 196616 | tf_op jit(solution)/shard_map/ppermute | solution.py:22
  70.0 0.9 %collective-permute-done.23 = bf16[256,128]{1,0:T(8,128)(2,1)S(1)} collective-permute-done((bf16[256,128]{1,0:T(8,128)(2,1)S(1)}, bf16[256,128]{1,0:T(8,128)(2,1)S(1)}, u32[]{:S(2)}, u32[]{:S(2)}) %collective-permute-start.23) | collective-permute-done | bytes 65568 | tf_op jit(solution)/shard_map/ppermute | solution.py:22
  70.9 1.8 %collective-permute-done.24 = bf16[256,128]{1,0:T(8,128)(2,1)S(1)} collective-permute-done((bf16[256,128]{1,0:T(8,128)(2,1)S(1)}, bf16[256,128]{1,0:T(8,128)(2,1)S(1)}, u32[]{:S(2)}, u32[]{:S(2)}) %collective-permute-start.24) | collective-permute-done | bytes 65568 | tf_op jit(solution)/shard_map/ppermute | solution.py:22
  73.3 1.7 %collective-permute-start.28 = (bf16[256,128]{1,0:T(8,128)(2,1)S(1)}, bf16[256,128]{1,0:T(8,128)(2,1)S(1)}, u32[]{:S(2)}, u32[]{:S(2)}) collective-permute-start(bf16[256,128]{1,0:T(8,128)(2,1)S(1)} %fusion.3.refs_0_), channel_id=1, source_target_pairs={{0,8},{8,0},{16,24},{24,16},{1,9},{9,1},{17,25},{25,17},{2,10},{10... | collective-permute-start | bytes 196616 | tf_op jit(solution)/shard_map/ppermute | solution.py:22
  75.0 1.7 %shard_map.86.lag_ref = f32[9,2,512,128]{3,2,1,0:T(8,128)S(1)} custom-call(bf16[1024,256]{1,0:T(8,128)(2,1)S(1)} %copy-done, bf16[2,512,128]{2,1,0:T(8,128)(2,1)S(1)} %pad_maximum_fusion.3.refs_0_, bf16[2,512,128]{2,1,0:T(8,128)(2,1)S(1)} %collective-permute-done.refs_1_, bf16[2,512,128]{2,1,0:T(8,128)(2,1)S(1)} %collective-permute-done.1.refs_2_, ...), custom_call_target="tpu_custom_call" | custom-call | flops 1073741824 | bytes 6291456 | tf_op jit(solution)/shard_map/pallas_call | solution.py:174
  77.3 0.8 %collective-permute-start.27 = (bf16[256,128]{1,0:T(8,128)(2,1)S(1)}, bf16[256,128]{1,0:T(8,128)(2,1)S(1)}, u32[]{:S(2)}, u32[]{:S(2)}) collective-permute-start(bf16[256,128]{1,0:T(8,128)(2,1)S(1)} %fusion.3.refs_0_), channel_id=1, source_target_pairs={{0,24},{8,16},{16,8},{24,0},{1,25},{9,17},{17,9},{25,1},{2,26},{10... | collective-permute-start | bytes 196616 | tf_op jit(solution)/shard_map/ppermute | solution.py:22
  78.2 1.2 %shard_map.91.refs_2_ = f32[512,512]{1,0:T(8,128)S(1)} custom-call(bf16[1024,256]{1,0:T(8,128)(2,1)S(1)} %copy-done, f32[9,2,512,128]{3,2,1,0:T(8,128)S(1)} %shard_map.86.lag_ref, bf16[256,128]{1,0:T(8,128)(2,1)S(1)} %fusion.7.refs_0_, bf16[256,128]{1,0:T(8,128)(2,1)S(1)} %collective-permute-done.29.refs_1_, ...), custom_call_target="tpu_custom_call" | custom-call | flops 536870912 | bytes 4194304 | tf_op jit(solution)/shard_map/pallas_call | solution.py:252
  80.0 1.7 %collective-permute-done.26.refs_0_ = bf16[256,128]{1,0:T(8,128)(2,1)S(1)} collective-permute-done((bf16[256,128]{1,0:T(8,128)(2,1)S(1)}, bf16[256,128]{1,0:T(8,128)(2,1)S(1)}, u32[]{:S(2)}, u32[]{:S(2)}) %collective-permute-start.26) | collective-permute-done | bytes 65568 | tf_op jit(solution)/shard_map/ppermute | solution.py:22
  81.7 1.7 %shard_map.93 = (bf16[512,128]{1,0:T(8,128)(2,1)}, f32[512,128]{1,0:T(8,128)}) custom-call(bf16[1024,256]{1,0:T(8,128)(2,1)S(1)} %copy-done, f32[9,2,512,128]{3,2,1,0:T(8,128)S(1)} %shard_map.86.lag_ref, bf16[256,128]{1,0:T(8,128)(2,1)S(1)} %collective-permute-done.26.refs_0_, bf16[256,128]{1,0:T(8,128)(2,1)S(1)} %collective-permute-done.27.refs_1_, ...), custom_call_target="tpu_custom_call" | custom-call | flops 268435456 | bytes 4194304 | tf_op jit(solution)/shard_map/pallas_call | solution.py:252
  (66 shorter events, 7.1 us)
Async XLA Ops:
  2.1 8.7 %collective-permute-start.8 = (bf16[128,256]{1,0:T(8,128)(2,1)S(1)}, bf16[128,256]{1,0:T(8,128)(2,1)S(1)}, u32[]{:S(2)}, u32[]{:S(2)}) collective-permute-start(bf16[128,256]{1,0:T(8,128)(2,1)S(1)} %get-tuple-element.29), channel_id=1, source_target_pairs={{0,5},{1,4},{2,7},{3,6},{4,1},{5,0},{6,3},{7,2},{8,13},{9,12},{10,... | collective-permute-start | bytes 196616 | tf_op jit(solution)/shard_map/ppermute | solution.py:22
  7.1 9.0 %collective-permute-start.6 = (bf16[128,256]{1,0:T(8,128)(2,1)S(1)}, bf16[128,256]{1,0:T(8,128)(2,1)S(1)}, u32[]{:S(2)}, u32[]{:S(2)}) collective-permute-start(bf16[128,256]{1,0:T(8,128)(2,1)S(1)} %get-tuple-element.28), channel_id=1, source_target_pairs={{0,7},{1,6},{2,5},{3,4},{4,3},{5,2},{6,1},{7,0},{8,15},{9,14},{10,... | collective-permute-start | bytes 196616 | tf_op jit(solution)/shard_map/ppermute | solution.py:22
  10.8 5.9 %collective-permute-start.9 = (bf16[128,256]{1,0:T(8,128)(2,1)S(1)}, bf16[128,256]{1,0:T(8,128)(2,1)S(1)}, u32[]{:S(2)}, u32[]{:S(2)}) collective-permute-start(bf16[128,256]{1,0:T(8,128)(2,1)S(1)} %collective-permute-done.8), channel_id=1, source_target_pairs={{0,16},{8,24},{16,0},{24,8},{1,17},{9,25},{17,1},{25,9},{2,18},{10... | collective-permute-start | bytes 196616 | tf_op jit(solution)/shard_map/ppermute | solution.py:22
  12.4 6.0 %collective-permute-start.12 = (bf16[128,512]{1,0:T(8,128)(2,1)S(1)}, bf16[128,512]{1,0:T(8,128)(2,1)S(1)}, u32[]{:S(2)}, u32[]{:S(2)}) collective-permute-start(bf16[128,512]{1,0:T(8,128)(2,1)S(1)} %get-tuple-element.30), channel_id=1, source_target_pairs={{0,3},{1,2},{2,1},{3,0},{4,7},{5,6},{6,5},{7,4},{8,11},{9,10},{10,... | collective-permute-start | bytes 393224 | tf_op jit(solution)/shard_map/ppermute | solution.py:22
  14.5 5.3 %collective-permute-start.13 = (bf16[128,512]{1,0:T(8,128)(2,1)S(1)}, bf16[128,512]{1,0:T(8,128)(2,1)S(1)}, u32[]{:S(2)}, u32[]{:S(2)}) collective-permute-start(bf16[128,512]{1,0:T(8,128)(2,1)S(1)} %get-tuple-element.31), channel_id=1, source_target_pairs={{0,1},{1,0},{2,3},{3,2},{4,5},{5,4},{6,7},{7,6},{8,9},{9,8},{10,11... | collective-permute-start | bytes 393224 | tf_op jit(solution)/shard_map/ppermute | solution.py:22
  16.1 4.3 %collective-permute-start.7 = (bf16[128,256]{1,0:T(8,128)(2,1)S(1)}, bf16[128,256]{1,0:T(8,128)(2,1)S(1)}, u32[]{:S(2)}, u32[]{:S(2)}) collective-permute-start(bf16[128,256]{1,0:T(8,128)(2,1)S(1)} %collective-permute-done.6), channel_id=1, source_target_pairs={{0,16},{8,24},{16,0},{24,8},{1,17},{9,25},{17,1},{25,9},{2,18},{10... | collective-permute-start | bytes 196616 | tf_op jit(solution)/shard_map/ppermute | solution.py:22
  16.7 9.8 %collective-permute-start.11 = (bf16[2,128,256]{2,1,0:T(8,128)(2,1)S(1)}, bf16[2,128,256]{2,1,0:T(8,128)(2,1)S(1)}, u32[]{:S(2)}, u32[]{:S(2)}) collective-permute-start(bf16[2,128,256]{2,1,0:T(8,128)(2,1)S(1)} %get-tuple-element.54), channel_id=1, source_target_pairs={{0,8},{8,0},{16,24},{24,16},{1,9},{9,1},{17,25},{25,17},{2,10},{10... | collective-permute-start | bytes 393224 | tf_op jit(solution)/shard_map/ppermute | solution.py:22
  19.8 7.4 %collective-permute-start.14 = (bf16[2,128,512]{2,1,0:T(8,128)(2,1)S(1)}, bf16[2,128,512]{2,1,0:T(8,128)(2,1)S(1)}, u32[]{:S(2)}, u32[]{:S(2)}) collective-permute-start(bf16[2,128,512]{2,1,0:T(8,128)(2,1)S(1)} %pad_maximum_fusion.6.refs_4_), channel_id=1, source_target_pairs={{0,8},{8,0},{16,24},{24,16},{1,9},{9,1},{17,25},{25,17},{2,10},{10... | collective-permute-start | bytes 786440 | tf_op jit(solution)/shard_map/ppermute | solution.py:22
  20.4 6.7 %collective-permute-start.10 = (bf16[2,128,256]{2,1,0:T(8,128)(2,1)S(1)}, bf16[2,128,256]{2,1,0:T(8,128)(2,1)S(1)}, u32[]{:S(2)}, u32[]{:S(2)}) collective-permute-start(bf16[2,128,256]{2,1,0:T(8,128)(2,1)S(1)} %get-tuple-element.52), channel_id=1, source_target_pairs={{0,8},{8,0},{16,24},{24,16},{1,9},{9,1},{17,25},{25,17},{2,10},{10... | collective-permute-start | bytes 393224 | tf_op jit(solution)/shard_map/ppermute | solution.py:22
  20.5 8.9 %collective-permute-start.3 = (bf16[128,512]{1,0:T(8,128)(2,1)S(1)}, bf16[128,512]{1,0:T(8,128)(2,1)S(1)}, u32[]{:S(2)}, u32[]{:S(2)}) collective-permute-start(bf16[128,512]{1,0:T(8,128)(2,1)S(1)} %get-tuple-element.25), channel_id=1, source_target_pairs={{0,6},{1,7},{2,4},{3,5},{4,2},{5,3},{6,0},{7,1},{8,14},{9,15},{10,... | collective-permute-start | bytes 393224 | tf_op jit(solution)/shard_map/ppermute | solution.py:22
  25.1 12.2 %collective-permute-start.4 = (bf16[128,512]{1,0:T(8,128)(2,1)S(1)}, bf16[128,512]{1,0:T(8,128)(2,1)S(1)}, u32[]{:S(2)}, u32[]{:S(2)}) collective-permute-start(bf16[128,512]{1,0:T(8,128)(2,1)S(1)} %get-tuple-element.26), channel_id=1, source_target_pairs={{0,4},{1,5},{2,6},{3,7},{4,0},{5,1},{6,2},{7,3},{8,12},{9,13},{10,... | collective-permute-start | bytes 393224 | tf_op jit(solution)/shard_map/ppermute | solution.py:22
  26.5 10.8 %collective-permute-start.5 = (bf16[128,512]{1,0:T(8,128)(2,1)S(1)}, bf16[128,512]{1,0:T(8,128)(2,1)S(1)}, u32[]{:S(2)}, u32[]{:S(2)}) collective-permute-start(bf16[128,512]{1,0:T(8,128)(2,1)S(1)} %get-tuple-element.27), channel_id=1, source_target_pairs={{0,2},{1,3},{2,0},{3,1},{4,6},{5,7},{6,4},{7,5},{8,10},{9,11},{10,... | collective-permute-start | bytes 393224 | tf_op jit(solution)/shard_map/ppermute | solution.py:22
  37.4 11.0 %collective-permute-start.15 = (bf16[3,128,512]{2,1,0:T(8,128)(2,1)S(1)}, bf16[3,128,512]{2,1,0:T(8,128)(2,1)S(1)}, u32[]{:S(2)}, u32[]{:S(2)}) collective-permute-start(bf16[3,128,512]{2,1,0:T(8,128)(2,1)S(1)} %pad_maximum_fusion.2), channel_id=1, source_target_pairs={{0,8},{8,0},{16,24},{24,16},{1,9},{9,1},{17,25},{25,17},{2,10},{10... | collective-permute-start | bytes 1179656 | tf_op jit(solution)/shard_map/ppermute | solution.py:22
  37.5 8.7 %collective-permute-start.1 = (bf16[2,512,128]{2,1,0:T(8,128)(2,1)S(1)}, bf16[2,512,128]{2,1,0:T(8,128)(2,1)S(1)}, u32[]{:S(2)}, u32[]{:S(2)}) collective-permute-start(bf16[2,512,128]{2,1,0:T(8,128)(2,1)S(1)} %pad_maximum_fusion.3.refs_0_), channel_id=1, source_target_pairs={{0,16},{8,24},{16,0},{24,8},{1,17},{9,25},{17,1},{25,9},{2,18},{10... | collective-permute-start | bytes 786440 | tf_op jit(solution)/shard_map/ppermute | solution.py:22
  38.1 35.2 %collective-permute-start = (bf16[2,512,128]{2,1,0:T(8,128)(2,1)S(1)}, bf16[2,512,128]{2,1,0:T(8,128)(2,1)S(1)}, u32[]{:S(2)}, u32[]{:S(2)}) collective-permute-start(bf16[2,512,128]{2,1,0:T(8,128)(2,1)S(1)} %pad_maximum_fusion.3.refs_0_), channel_id=1, source_target_pairs={{0,8},{8,0},{16,24},{24,16},{1,9},{9,1},{17,25},{25,17},{2,10},{10... | collective-permute-start | bytes 786440 | tf_op jit(solution)/shard_map/ppermute | solution.py:22
  46.3 28.7 %collective-permute-start.2 = (bf16[2,512,128]{2,1,0:T(8,128)(2,1)S(1)}, bf16[2,512,128]{2,1,0:T(8,128)(2,1)S(1)}, u32[]{:S(2)}, u32[]{:S(2)}) collective-permute-start(bf16[2,512,128]{2,1,0:T(8,128)(2,1)S(1)} %collective-permute-done.1.refs_2_), channel_id=1, source_target_pairs={{0,8},{8,0},{16,24},{24,16},{1,9},{9,1},{17,25},{25,17},{2,10},{10... | collective-permute-start | bytes 786440 | tf_op jit(solution)/shard_map/ppermute | solution.py:22
  46.3 6.4 %collective-permute-start.17 = (bf16[2,256,128]{2,1,0:T(8,128)(2,1)S(1)}, bf16[2,256,128]{2,1,0:T(8,128)(2,1)S(1)}, u32[]{:S(2)}, u32[]{:S(2)}) collective-permute-start(bf16[2,256,128]{2,1,0:T(8,128)(2,1)S(1)} %get-tuple-element.32), channel_id=1, source_target_pairs={{0,1},{1,0},{2,3},{3,2},{4,5},{5,4},{6,7},{7,6},{8,9},{9,8},{10,11... | collective-permute-start | bytes 393224 | tf_op jit(solution)/shard_map/ppermute | solution.py:22
  46.8 14.1 %collective-permute-start.16 = (bf16[2,256,128]{2,1,0:T(8,128)(2,1)S(1)}, bf16[2,256,128]{2,1,0:T(8,128)(2,1)S(1)}, u32[]{:S(2)}, u32[]{:S(2)}) collective-permute-start(bf16[2,256,128]{2,1,0:T(8,128)(2,1)S(1)} %get-tuple-element.39), channel_id=1, source_target_pairs={{0,1},{1,0},{2,3},{3,2},{4,5},{5,4},{6,7},{7,6},{8,9},{9,8},{10,11... | collective-permute-start | bytes 393224 | tf_op jit(solution)/shard_map/ppermute | solution.py:22
  48.4 9.9 %collective-permute-start.22 = (bf16[2,256,128]{2,1,0:T(8,128)(2,1)S(1)}, bf16[2,256,128]{2,1,0:T(8,128)(2,1)S(1)}, u32[]{:S(2)}, u32[]{:S(2)}) collective-permute-start(bf16[2,256,128]{2,1,0:T(8,128)(2,1)S(1)} %get-tuple-element.45), channel_id=1, source_target_pairs={{0,1},{1,0},{2,3},{3,2},{4,5},{5,4},{6,7},{7,6},{8,9},{9,8},{10,11... | collective-permute-start | bytes 393224 | tf_op jit(solution)/shard_map/ppermute | solution.py:22
  52.6 8.5 %collective-permute-start.21 = (bf16[2,256,128]{2,1,0:T(8,128)(2,1)S(1)}, bf16[2,256,128]{2,1,0:T(8,128)(2,1)S(1)}, u32[]{:S(2)}, u32[]{:S(2)}) collective-permute-start(bf16[2,256,128]{2,1,0:T(8,128)(2,1)S(1)} %get-tuple-element.43), channel_id=1, source_target_pairs={{0,1},{1,0},{2,3},{3,2},{4,5},{5,4},{6,7},{7,6},{8,9},{9,8},{10,11... | collective-permute-start | bytes 393224 | tf_op jit(solution)/shard_map/ppermute | solution.py:22
  58.2 6.2 %collective-permute-start.18 = (bf16[256,128]{1,0:T(8,128)(2,1)S(1)}, bf16[256,128]{1,0:T(8,128)(2,1)S(1)}, u32[]{:S(2)}, u32[]{:S(2)}) collective-permute-start(bf16[256,128]{1,0:T(8,128)(2,1)S(1)} %get-tuple-element.50), channel_id=1, source_target_pairs={{0,6},{1,7},{2,4},{3,5},{4,2},{5,3},{6,0},{7,1},{8,14},{9,15},{10,... | collective-permute-start | bytes 196616 | tf_op jit(solution)/shard_map/ppermute | solution.py:22
  61.0 6.4 %collective-permute-start.19 = (bf16[256,128]{1,0:T(8,128)(2,1)S(1)}, bf16[256,128]{1,0:T(8,128)(2,1)S(1)}, u32[]{:S(2)}, u32[]{:S(2)}) collective-permute-start(bf16[256,128]{1,0:T(8,128)(2,1)S(1)} %get-tuple-element.51), channel_id=1, source_target_pairs={{0,4},{1,5},{2,6},{3,7},{4,0},{5,1},{6,2},{7,3},{8,12},{9,13},{10,... | collective-permute-start | bytes 196616 | tf_op jit(solution)/shard_map/ppermute | solution.py:22
  61.1 6.3 %collective-permute-start.20 = (bf16[256,128]{1,0:T(8,128)(2,1)S(1)}, bf16[256,128]{1,0:T(8,128)(2,1)S(1)}, u32[]{:S(2)}, u32[]{:S(2)}) collective-permute-start(bf16[256,128]{1,0:T(8,128)(2,1)S(1)} %fusion.10), channel_id=1, source_target_pairs={{0,2},{1,3},{2,0},{3,1},{4,6},{5,7},{6,4},{7,5},{8,10},{9,11},{10,... | collective-permute-start | bytes 196616 | tf_op jit(solution)/shard_map/ppermute | solution.py:22
  64.5 6.4 %collective-permute-start.23 = (bf16[256,128]{1,0:T(8,128)(2,1)S(1)}, bf16[256,128]{1,0:T(8,128)(2,1)S(1)}, u32[]{:S(2)}, u32[]{:S(2)}) collective-permute-start(bf16[256,128]{1,0:T(8,128)(2,1)S(1)} %get-tuple-element.48), channel_id=1, source_target_pairs={{0,6},{1,7},{2,4},{3,5},{4,2},{5,3},{6,0},{7,1},{8,14},{9,15},{10,... | collective-permute-start | bytes 196616 | tf_op jit(solution)/shard_map/ppermute | solution.py:22
  67.4 5.3 %collective-permute-start.24 = (bf16[256,128]{1,0:T(8,128)(2,1)S(1)}, bf16[256,128]{1,0:T(8,128)(2,1)S(1)}, u32[]{:S(2)}, u32[]{:S(2)}) collective-permute-start(bf16[256,128]{1,0:T(8,128)(2,1)S(1)} %get-tuple-element.49), channel_id=1, source_target_pairs={{0,4},{1,5},{2,6},{3,7},{4,0},{5,1},{6,2},{7,3},{8,12},{9,13},{10,... | collective-permute-start | bytes 196616 | tf_op jit(solution)/shard_map/ppermute | solution.py:22
  67.4 5.8 %collective-permute-start.25 = (bf16[256,128]{1,0:T(8,128)(2,1)S(1)}, bf16[256,128]{1,0:T(8,128)(2,1)S(1)}, u32[]{:S(2)}, u32[]{:S(2)}) collective-permute-start(bf16[256,128]{1,0:T(8,128)(2,1)S(1)} %fusion.13), channel_id=1, source_target_pairs={{0,2},{1,3},{2,0},{3,1},{4,6},{5,7},{6,4},{7,5},{8,10},{9,11},{10,... | collective-permute-start | bytes 196616 | tf_op jit(solution)/shard_map/ppermute | solution.py:22
  70.9 6.4 %collective-permute-start.29 = (bf16[256,128]{1,0:T(8,128)(2,1)S(1)}, bf16[256,128]{1,0:T(8,128)(2,1)S(1)}, u32[]{:S(2)}, u32[]{:S(2)}) collective-permute-start(bf16[256,128]{1,0:T(8,128)(2,1)S(1)} %fusion.7.refs_0_), channel_id=1, source_target_pairs={{0,8},{8,0},{16,24},{24,16},{1,9},{9,1},{17,25},{25,17},{2,10},{10... | collective-permute-start | bytes 196616 | tf_op jit(solution)/shard_map/ppermute | solution.py:22
  72.7 5.4 %collective-permute-start.30 = (bf16[256,128]{1,0:T(8,128)(2,1)S(1)}, bf16[256,128]{1,0:T(8,128)(2,1)S(1)}, u32[]{:S(2)}, u32[]{:S(2)}) collective-permute-start(bf16[256,128]{1,0:T(8,128)(2,1)S(1)} %fusion.7.refs_0_), channel_id=1, source_target_pairs={{0,16},{8,24},{16,0},{24,8},{1,17},{9,25},{17,1},{25,9},{2,18},{10... | collective-permute-start | bytes 196616 | tf_op jit(solution)/shard_map/ppermute | solution.py:22
  73.2 4.9 %collective-permute-start.31 = (bf16[256,128]{1,0:T(8,128)(2,1)S(1)}, bf16[256,128]{1,0:T(8,128)(2,1)S(1)}, u32[]{:S(2)}, u32[]{:S(2)}) collective-permute-start(bf16[256,128]{1,0:T(8,128)(2,1)S(1)} %fusion.7.refs_0_), channel_id=1, source_target_pairs={{0,24},{8,16},{16,8},{24,0},{1,25},{9,17},{17,9},{25,1},{2,26},{10... | collective-permute-start | bytes 196616 | tf_op jit(solution)/shard_map/ppermute | solution.py:22
  73.3 6.1 %collective-permute-start.28 = (bf16[256,128]{1,0:T(8,128)(2,1)S(1)}, bf16[256,128]{1,0:T(8,128)(2,1)S(1)}, u32[]{:S(2)}, u32[]{:S(2)}) collective-permute-start(bf16[256,128]{1,0:T(8,128)(2,1)S(1)} %fusion.3.refs_0_), channel_id=1, source_target_pairs={{0,8},{8,0},{16,24},{24,16},{1,9},{9,1},{17,25},{25,17},{2,10},{10... | collective-permute-start | bytes 196616 | tf_op jit(solution)/shard_map/ppermute | solution.py:22
  76.7 5.0 %collective-permute-start.26 = (bf16[256,128]{1,0:T(8,128)(2,1)S(1)}, bf16[256,128]{1,0:T(8,128)(2,1)S(1)}, u32[]{:S(2)}, u32[]{:S(2)}) collective-permute-start(bf16[256,128]{1,0:T(8,128)(2,1)S(1)} %fusion.3.refs_0_), channel_id=1, source_target_pairs={{0,16},{8,24},{16,0},{24,8},{1,17},{9,25},{17,1},{25,9},{2,18},{10... | collective-permute-start | bytes 196616 | tf_op jit(solution)/shard_map/ppermute | solution.py:22
  77.3 4.4 %collective-permute-start.27 = (bf16[256,128]{1,0:T(8,128)(2,1)S(1)}, bf16[256,128]{1,0:T(8,128)(2,1)S(1)}, u32[]{:S(2)}, u32[]{:S(2)}) collective-permute-start(bf16[256,128]{1,0:T(8,128)(2,1)S(1)} %fusion.3.refs_0_), channel_id=1, source_target_pairs={{0,24},{8,16},{16,8},{24,0},{1,25},{9,17},{17,9},{25,1},{2,26},{10... | collective-permute-start | bytes 196616 | tf_op jit(solution)/shard_map/ppermute | solution.py:22
  (5 other events, 163.0 us)
